TPU v7x, 128 devices: a whole 4x4x4 slice. The times are simulated.
128 devices in a mesh: grid: 16 (over x, y), dom: 8 (over z, core).
Axes of the slice: x: 4, y: 4, z: 4, core: 2. Of those that a mesh axis runs over, the one named last changes fastest.
Arguments:
- concentration: float32 [16, 128, 8192], P('grid', 'dom'), may hold values from -6 to 6
- diffusion: float32 [16, 128, 8192], P('grid', 'dom'), may hold values from 0.25 to 1
- velocity: float32 [4], replicated, may hold values from -1 to 1
- levels: int32 [16, 3], P('grid'), may hold values from 3 to 7, as said below
- grid_signs: int32 [16], P('grid'), may hold values from -1 to 1, as said below
- owner_list: int32 [128, 128], P(('grid', 'dom')), may hold values from 0 to 127, as said below
- slot_list: int32 [128, 128], P(('grid', 'dom')), may hold values from 0 to 63
Outputs:
- combined: float32 [16, 128, 8192], P('grid', 'dom')
Inputs may be any that keep to these rules, and one draw needn't show every extreme that they name: Each row's three levels sum to 13. `grid_signs`: each is -1 or 1. `owner_list`: at most 2 blocks of one device name the same owner; some owner is named by 2 blocks of every device.
All inputs are finite; a program needn't handle non-finite values.
Results may differ from a plain program's by a relative error of at most 0.0003.
Values sent between devices are 32-bit elements; how exact they have to be, the bound alone decides.
A program may use at most 192 MiB of HBM per device.

v0:
```python
import jax
import jax.numpy as jnp
from jax import lax
from jax.experimental import pallas as pl
from jax.experimental.pallas import tpu as pltpu
from jax.sharding import PartitionSpec as P

MESH = pl.DeviceIdType.MESH
F32 = jnp.float32
BF16 = jnp.bfloat16
I32 = jnp.int32

COLS = 64
PAD = 8
TILE_HALO = PAD + 2 * COLS


def tile(at):
    return pl.ds(at * 8, 8)


def node_rows(base, node):
    return pl.ds(base + (node // 8) * COLS * 8 + node % 8, COLS, stride=8)


def dot_exact(left, right):
    first = left.astype(BF16)
    rest = left - first.astype(F32)
    second = rest.astype(BF16)
    third = (rest - second.astype(F32)).astype(BF16)
    total = jnp.dot(third, right, preferred_element_type=F32)
    total = total + jnp.dot(second, right, preferred_element_type=F32)
    return total + jnp.dot(first, right, preferred_element_type=F32)


def lane_matrices(l1, l2, sign):
    source = lax.broadcasted_iota(I32, (128, 128), 0)
    target = lax.broadcasted_iota(I32, (128, 128), 1)
    both = l1 + l2
    low = [0, l1, both]
    top = [jnp.minimum(l1, 7), jnp.minimum(both, 7), 7]
    here = jnp.full((128, 128), sign, F32)
    after = jnp.full((128, 128), sign, F32)
    for field in range(3):
        width = jnp.maximum(top[field] - jnp.minimum(low[field], 7), 0)
        mask = jnp.left_shift(1, width) - 1
        shift = jnp.minimum(low[field], 7)
        fro = jnp.right_shift(source, shift) & mask
        to = jnp.right_shift(target, shift) & mask
        bit = to & (-to)
        same = jnp.where(fro == to, 1.0, 0.0)
        near = jnp.where((to != 0) & ((fro == to - bit) | (fro == to + bit)), -0.5, 0.0)
        plain = same + near
        wraps = (to != 0) & (to + bit == mask + 1) & (fro == 0)
        carry = jnp.where(wraps, -0.5, 0.0)
        here = here * plain
        if field == 0:
            after = after * plain
        elif field == 1:
            after = after * jnp.where(both > 6, jnp.where(width > 0, carry, 0.0), plain)
        else:
            after = after * jnp.where(both > 6, 1.0, carry)
    return here, after


def surplus_kernel(
    lev_ref, vel_ref, sign_ref, u_hbm, k_hbm, s_ref,
    start, mid, coef, stepped, lanes_done, rows_done, packs, low_in, high_in, lead, lead_in,
    load_sem, send_sem, recv_sem, lead_send, lead_recv,
):
    g = lax.axis_index("grid")
    d = lax.axis_index("dom")
    barrier = pltpu.get_barrier_semaphore()
    for k in range(1, 8):
        pl.semaphore_signal(
            barrier, inc=1, device_id=(g, lax.rem(d + k, 8)), device_id_type=MESH
        )
    load_u = pltpu.make_async_copy(u_hbm, start.at[pl.ds(PAD * 8, 1024)], load_sem.at[0])
    load_k = pltpu.make_async_copy(k_hbm, coef.at[pl.ds(0, 1024)], load_sem.at[1])
    load_u.start()
    load_k.start()
    zero_pad = jnp.zeros((PAD * 8, 128), F32)
    for buffer in (start, mid):
        buffer[0 : PAD * 8] = zero_pad
        buffer[(TILE_HALO + COLS) * 8 : (TILE_HALO + COLS + PAD) * 8] = zero_pad
    load_u.wait()
    load_k.wait()
    base = PAD * 8
    packs[0, 0:64] = start[node_rows(base, 0), :]
    packs[0, 64:128] = start[node_rows(base, 1), :]
    packs[0, 128:192] = coef[node_rows(0, 0), :]
    packs[1, 0:64] = start[node_rows(base, 14), :]
    packs[1, 64:128] = start[node_rows(base, 15), :]
    packs[1, 128:192] = coef[node_rows(0, 15), :]
    pl.semaphore_wait(barrier, 7)

    def down():
        return pltpu.make_async_remote_copy(
            src_ref=packs.at[0], dst_ref=high_in, send_sem=send_sem.at[0], recv_sem=recv_sem.at[0],
            device_id=(g, lax.rem(d + 7, 8)), device_id_type=MESH,
        )

    def upward():
        return pltpu.make_async_remote_copy(
            src_ref=packs.at[1], dst_ref=low_in, send_sem=send_sem.at[1], recv_sem=recv_sem.at[1],
            device_id=(g, lax.rem(d + 1, 8)), device_id_type=MESH,
        )

    @pl.when(d > 0)
    def _():
        down().start()

    @pl.when(d < 7)
    def _():
        upward().start()

    zero_rows = jnp.zeros((192, 128), F32)

    @pl.when(d == 0)
    def _():
        low_in[...] = zero_rows

    @pl.when(d == 7)
    def _():
        high_in[...] = zero_rows

    l1 = lev_ref[0, 0]
    l2 = lev_ref[0, 1]
    l3 = lev_ref[0, 2]
    both = l1 + l2
    lane = lax.broadcasted_iota(I32, (8, 128), 1)
    sub = lax.broadcasted_iota(I32, (8, 128), 0)
    span2 = jnp.left_shift(1, l1)
    span3 = jnp.minimum(jnp.left_shift(1, both), 128)
    skip3 = jnp.where(both == 8, 2, jnp.where(both == 9, 4, jnp.where(both == 10, 8, 1)))
    last1 = jnp.left_shift(1, l1) - 1
    last2 = jnp.left_shift(1, l2) - 1
    last3 = jnp.left_shift(1, l3) - 1
    drift1 = 0.1 * vel_ref[0]
    drift2 = 0.1 * vel_ref[1]
    drift3 = 0.1 * vel_ref[2]
    drift4 = 0.1 * vel_ref[3]
    from_next2 = lane < span2
    from_last2 = lane >= 128 - span2
    from_next3 = lane < span3
    from_last3 = lane >= 128 - span3
    ahead2 = (128 - span2) & 127
    behind2 = span2 & 127
    ahead3 = (128 - span3) & 127
    behind3 = span3 & 127

    def masks(c):
        cell = c * 128 + lane
        i1 = cell & last1
        i2 = jnp.right_shift(cell, l1) & last2
        i3 = jnp.right_shift(cell, both) & last3
        return (i1 != last1, i1 != 0, i2 != last2, i2 != 0, i3 != last3, i3 != 0)

    def advance(ref, at, x, ahead4, behind4, diff, ok):
        p1 = jnp.where(ok[0], pltpu.roll(x, 127, 1), 0.0)
        m1 = jnp.where(ok[1], pltpu.roll(x, 1, 1), 0.0)
        p2 = pltpu.roll(jnp.where(from_next2, ref[tile(at + 1), :], x), ahead2, 1)
        p2 = jnp.where(ok[2], p2, 0.0)
        m2 = pltpu.roll(jnp.where(from_last2, ref[tile(at - 1), :], x), behind2, 1)
        m2 = jnp.where(ok[3], m2, 0.0)
        p3 = pltpu.roll(jnp.where(from_next3, ref[tile(at + skip3), :], x), ahead3, 1)
        p3 = jnp.where(ok[4], p3, 0.0)
        m3 = pltpu.roll(jnp.where(from_last3, ref[tile(at - skip3), :], x), behind3, 1)
        m3 = jnp.where(ok[5], m3, 0.0)
        second = ((p1 + m1) + (p2 + m2)) + ((p3 + m3) + (ahead4 + behind4)) - 8.0 * x
        drift = (drift1 * (p1 - m1) + drift2 * (p2 - m2)) + (
            drift3 * (p3 - m3) + drift4 * (ahead4 - behind4)
        )
        return x + 0.1 * diff * second - drift

    def both_groups(ref, c, write):
        ok = masks(c)
        x0 = ref[tile(PAD + c), :]
        x1 = ref[tile(PAD + COLS + c), :]
        xh = ref[tile(TILE_HALO + c), :]
        before = pltpu.roll(xh, 6, 0)
        after = pltpu.roll(xh, 2, 0)
        write(0, c, advance(
            ref, PAD + c, x0, pltpu.roll(jnp.where(sub == 0, x1, x0), 7, 0),
            pltpu.roll(jnp.where(sub == 7, before, x0), 1, 0), coef[tile(c), :], ok,
        ))
        write(1, c, advance(
            ref, PAD + COLS + c, x1, pltpu.roll(jnp.where(sub == 0, after, x1), 7, 0),
            pltpu.roll(jnp.where(sub == 7, x0, x1), 1, 0), coef[tile(COLS + c), :], ok,
        ))
        return xh, ok

    @pl.when(d < 7)
    def _():
        down().wait_recv()

    @pl.when(d > 0)
    def _():
        upward().wait_recv()

    halo = TILE_HALO * 8

    def halo_rows(s):
        return pl.ds(halo + s, COLS, stride=8)

    start[halo_rows(0), :] = low_in[0:64]
    start[halo_rows(1), :] = low_in[64:128]
    start[halo_rows(2), :] = packs[0, 0:64]
    start[halo_rows(3), :] = packs[0, 64:128]
    start[halo_rows(4), :] = packs[1, 0:64]
    start[halo_rows(5), :] = packs[1, 64:128]
    start[halo_rows(6), :] = high_in[0:64]
    start[halo_rows(7), :] = high_in[64:128]
    coef[1024:1536] = jnp.zeros((512, 128), F32)
    coef[pl.ds(1024 + 1, COLS, stride=8), :] = low_in[128:192]
    coef[pl.ds(1024 + 6, COLS, stride=8), :] = high_in[128:192]
    outside = jnp.where(d == 0, 1, jnp.where(d == 7, 6, -1))

    def write_mid(t, c, value):
        mid[tile(PAD + t * COLS + c), :] = value

    def first_step(c, carry):
        xh, ok = both_groups(start, c, write_mid)
        value = advance(
            start, TILE_HALO + c, xh, pltpu.roll(xh, 7, 0), pltpu.roll(xh, 1, 0),
            coef[tile(2 * COLS + c), :], ok,
        )
        mid[tile(TILE_HALO + c), :] = jnp.where(sub == outside, 0.0, value)
        return carry

    def write_stepped(t, c, value):
        stepped[tile(t * COLS + c), :] = value

    def second_step(c, carry):
        both_groups(mid, c, write_stepped)
        return carry

    lax.fori_loop(0, COLS, first_step, 0)
    lax.fori_loop(0, COLS, second_step, 0)

    here, after = lane_matrices(l1, l2, sign_ref[0].astype(F32))
    here = here.astype(BF16)
    after = after.astype(BF16)
    straddles = jnp.where(both > 7, jnp.where(l1 < 7, 1, 0), jnp.where(both == 6, 1, 0))
    mask_a = jnp.where(both > 7, skip3 - 1, COLS - 1)
    no_next = jnp.where(straddles == 1, mask_a, 0)
    limit_a = jnp.where(both > 7, span2, span3)
    mask_b = jnp.where(both > 7, COLS - skip3, 0)
    chunk = 128
    stepped[1024:1032] = jnp.zeros((8, 128), F32)

    def lane_part(i, carry):
        row = pl.multiple_of(i * chunk, chunk)
        x = stepped[pl.ds(row, chunk), :]
        beyond = stepped[pl.ds(pl.multiple_of(row + 8, 8), chunk), :]
        col = jnp.right_shift(row + lax.broadcasted_iota(I32, (chunk, 128), 0), 3)
        beyond = jnp.where((col & no_next) != no_next, beyond, 0.0)
        lanes_done[pl.ds(row, chunk), :] = dot_exact(x, here) + dot_exact(beyond, after)
        return carry

    lax.fori_loop(0, 1024 // chunk, lane_part, 0)

    def neighbours(c, mask):
        j = c & mask
        off = j & (-j)
        has_up = (j != 0) & (j + off <= mask)
        weight = jnp.where(j != 0, 0.5, 0.0)
        weight_up = jnp.where(has_up, 0.5, 0.0)
        return c - off, jnp.where(has_up, c + off, c), weight, weight_up

    inside = lane < limit_a

    def columns_a(c, carry):
        lower, upper, weight, weight_up = neighbours(c, mask_a)
        for t in range(2):
            at = t * COLS
            update = weight * lanes_done[tile(at + lower), :]
            update = update + weight_up * lanes_done[tile(at + upper), :]
            rows_done[tile(at + c), :] = lanes_done[tile(at + c), :] - jnp.where(
                inside, update, 0.0
            )
        return carry

    lax.fori_loop(0, COLS, columns_a, 0)

    def columns_b(c, carry):
        lower, upper, weight, weight_up = neighbours(c, mask_b)
        for t in range(2):
            at = t * COLS
            update = weight * rows_done[tile(at + lower), :]
            update = update + weight_up * rows_done[tile(at + upper), :]
            lanes_done[tile(at + c), :] = rows_done[tile(at + c), :] - update
        return carry

    lax.fori_loop(0, COLS, columns_b, 0)

    lead[...] = lanes_done[node_rows(0, 0), :]

    def lead_copy(slot, target, sent):
        return pltpu.make_async_remote_copy(
            src_ref=lead, dst_ref=lead_in.at[slot], send_sem=lead_send.at[sent],
            recv_sem=lead_recv.at[slot], device_id=(g, target), device_id_type=MESH,
        )

    routes = [(0, d > 0, lax.rem(d + 7, 8)), (1, lax.rem(d, 2) == 0, lax.rem(d + 1, 8))]
    routes += [(1, d == 0, 2), (1, d == 0, 4), (1, d == 4, 6), (2, d == 4, 2)]
    for sent, (slot, condition, target) in enumerate(routes):

        @pl.when(condition)
        def _():
            lead_copy(slot, target, sent).start()

    zero_lead = jnp.zeros((64, 128), F32)

    @pl.when(d == 7)
    def _():
        lead_in[0] = zero_lead

    @pl.when(d == 0)
    def _():
        lead_in[1] = zero_lead

    @pl.when(d != 2)
    def _():
        lead_in[2] = zero_lead

    @pl.when(d < 7)
    def _():
        lead_copy(0, lax.rem(d + 7, 8), 0).wait_recv()

    @pl.when(d > 0)
    def _():
        lead_copy(1, lax.rem(d + 1, 8), 0).wait_recv()

    @pl.when(d == 2)
    def _():
        lead_copy(2, lax.rem(d + 1, 8), 0).wait_recv()

    use_next = jnp.where(lax.rem(d, 2) == 1, 1.0, 0.0)
    odd = (sub & 1) == 1
    two = (sub & 3) == 2
    four = sub == 4

    def fourth(c, carry):
        x0 = lanes_done[tile(c), :]
        x1 = lanes_done[tile(COLS + c), :]
        following = jnp.broadcast_to(lead_in[0, pl.ds(c, 1), :], (8, 128))
        lower = jnp.broadcast_to(lead_in[1, pl.ds(c, 1), :], (8, 128))
        upper = jnp.broadcast_to(lead_in[2, pl.ds(c, 1), :], (8, 128)) + use_next * following
        upper = jnp.where(d > 0, upper, 0.0)
        for t, x, beyond, special in ((0, x0, x1, lower + upper), (1, x1, following, x0 + following)):
            y = jnp.where(sub == 0, beyond, x)
            near1 = pltpu.roll(y, 7, 0) + pltpu.roll(x, 1, 0)
            near2 = pltpu.roll(y, 6, 0) + pltpu.roll(x, 2, 0)
            near4 = pltpu.roll(y, 4, 0) + pltpu.roll(x, 4, 0)
            near = jnp.where(odd, near1, jnp.where(two, near2, jnp.where(four, near4, special)))
            s_ref[tile(t * COLS + c), :] = x - 0.5 * near
        return carry

    lax.fori_loop(0, COLS, fourth, 0)

    @pl.when(d > 0)
    def _():
        down().wait_send()

    @pl.when(d < 7)
    def _():
        upward().wait_send()

    for sent, (slot, condition, target) in enumerate(routes):

        @pl.when(condition)
        def _():
            lead_copy(slot, target, sent).wait_send()


def block_rows(block):
    node = lax.div(block, 8)
    at = (lax.div(node, 8) * COLS + lax.rem(block, 8) * 8) * 8 + lax.rem(node, 8)
    return pl.ds(at, 8, stride=8)


def exchange_kernel(
    s_ref, own_ref, slot_ref, out_ref,
    outgoing, arrived, returned, back, slots_out, slots_in, index_v, index_s,
    index_sem, send_sem, recv_sem,
):
    g = lax.axis_index("grid")
    d = lax.axis_index("dom")
    me = g * 8 + d
    x, y = lax.div(g, 4), lax.rem(g, 4)
    z, core = lax.div(d, 2), lax.rem(d, 2)
    barrier = pltpu.get_barrier_semaphore()

    def peer(k):
        px = lax.rem(x + lax.div(k, 32), 4)
        py = lax.rem(y + lax.rem(lax.div(k, 8), 4), 4)
        pz = lax.rem(z + lax.rem(lax.div(k, 2), 4), 4)
        pc = lax.rem(core + lax.rem(k, 2), 2)
        return px * 4 + py, pz * 2 + pc

    def greet(k, carry):
        pl.semaphore_signal(barrier, inc=1, device_id=peer(k), device_id_type=MESH)
        return carry

    lax.fori_loop(1, 128, greet, 0)

    owners = own_ref[...]
    slot_ids = slot_ref[...]
    own_row = jnp.broadcast_to(owners, (128, 128))
    own_col = own_row.T
    row = lax.broadcasted_iota(I32, (128, 128), 0)
    col = lax.broadcasted_iota(I32, (128, 128), 1)
    earlier = jnp.where((own_row == own_col) & (row < col), 1, 0)
    rank = jnp.sum(earlier, axis=0, keepdims=True)
    rank_row = jnp.broadcast_to(rank, (128, 128))
    rank_col = rank_row.T
    slot_row = jnp.broadcast_to(slot_ids, (128, 128))
    table = jnp.full((128, 128), -1, I32)
    index_v[...] = jnp.zeros((8, 128), I32)
    index_v[0:1] = 2 * owners + rank
    for r in range(2):
        to_owner = (own_col == col) & (rank_col == r)
        index_v[1 + r : 2 + r] = jnp.sum(jnp.where(to_owner, row, 0), axis=0, keepdims=True)
        of_block = (own_row == row) & (rank_row == r)
        ids = jnp.sum(jnp.where(of_block, slot_row + 1, 0), axis=1, keepdims=True) - 1
        table = jnp.where(col == r, ids, table)
    slots_out[:, 0, :] = table
    fetch = pltpu.make_async_copy(index_v, index_s, index_sem)
    fetch.start()
    fetch.wait()

    def pack(o, carry):
        for r in range(2):
            outgoing[tile(2 * o + r), :] = s_ref[block_rows(index_s[1 + r, o]), :]
        return carry

    lax.fori_loop(0, 128, pack, 0)
    pl.semaphore_wait(barrier, 127)

    def share(at):
        return pl.ds(pl.multiple_of(at * 16, 16), 16)

    def send(k, carry):
        pg, pd = peer(k)
        to = pg * 8 + pd
        pltpu.make_async_remote_copy(
            src_ref=slots_out.at[to], dst_ref=slots_in.at[me], send_sem=send_sem.at[0],
            recv_sem=recv_sem.at[0], device_id=(pg, pd), device_id_type=MESH,
        ).start()
        pltpu.make_async_remote_copy(
            src_ref=outgoing.at[share(to)], dst_ref=arrived.at[share(me)], send_sem=send_sem.at[1],
            recv_sem=recv_sem.at[1], device_id=(pg, pd), device_id_type=MESH,
        ).start()
        return carry

    lax.fori_loop(1, 128, send, 0)
    slots_in[me] = slots_out[me]
    arrived[share(me), :] = outgoing[share(me), :]
    anyone = (g, lax.rem(d + 1, 8))

    def all_of(source, target, which):
        size = 127 * (source.shape[0] // 128)
        return pltpu.make_async_remote_copy(
            src_ref=source.at[pl.ds(0, size)], dst_ref=target.at[pl.ds(0, size)],
            send_sem=send_sem.at[which], recv_sem=recv_sem.at[which],
            device_id=anyone, device_id_type=MESH,
        )

    all_of(slots_out, slots_in, 0).wait_recv()
    ids_col = slots_in[:, 0, :]
    ids_row = ids_col.T
    equal = jnp.concatenate(
        [
            jnp.concatenate(
                [
                    jnp.where(
                        jnp.broadcast_to(ids_col[:, r : r + 1], (128, 128))
                        == jnp.broadcast_to(ids_row[s : s + 1, :], (128, 128)),
                        1.0,
                        0.0,
                    )
                    for s in range(2)
                ],
                axis=1,
            )
            for r in range(2)
        ],
        axis=0,
    ).astype(BF16)
    all_of(outgoing, arrived, 1).wait_recv()
    for j in range(8):
        block = jnp.concatenate(
            [arrived[pl.ds(r * 8 + j, 128, stride=16), :] for r in range(2)], axis=0
        )
        first = block.astype(BF16)
        rest = block - first.astype(F32)
        second = rest.astype(BF16)
        third = (rest - second.astype(F32)).astype(BF16)
        total = jnp.dot(equal, third, preferred_element_type=F32)
        total = total + jnp.dot(equal, second, preferred_element_type=F32)
        total = total + jnp.dot(equal, first, preferred_element_type=F32)
        for r in range(2):
            returned[pl.ds(r * 8 + j, 128, stride=16), :] = total[r * 128 : (r + 1) * 128]

    def send_back(k, carry):
        pg, pd = peer(k)
        to = pg * 8 + pd
        pltpu.make_async_remote_copy(
            src_ref=returned.at[share(to)], dst_ref=back.at[share(me)], send_sem=send_sem.at[2],
            recv_sem=recv_sem.at[2], device_id=(pg, pd), device_id_type=MESH,
        ).start()
        return carry

    lax.fori_loop(1, 128, send_back, 0)
    back[share(me), :] = returned[share(me), :]
    all_of(returned, back, 2).wait_recv()

    def unpack(b, carry):
        out_ref[block_rows(b), :] = back[tile(index_s[0, b]), :]
        return carry

    lax.fori_loop(0, 128, unpack, 0)
    all_of(slots_out, slots_in, 0).wait_send()
    all_of(outgoing, arrived, 1).wait_send()
    all_of(returned, back, 2).wait_send()


def body(concentration, diffusion, velocity, levels, grid_signs, owner_list, slot_list):
    def tiled(block):
        return block.reshape(2, 8, COLS, 128).transpose(0, 2, 1, 3).reshape(1024, 128)

    smem = pl.BlockSpec(memory_space=pltpu.SMEM)
    vmem = pl.BlockSpec(memory_space=pltpu.VMEM)
    anywhere = pl.BlockSpec(memory_space=pl.ANY)
    total_rows = (TILE_HALO + COLS + PAD) * 8
    surplus = pl.pallas_call(
        surplus_kernel,
        out_shape=jax.ShapeDtypeStruct((1032, 128), F32),
        in_specs=[smem, smem, smem, anywhere, anywhere],
        out_specs=vmem,
        scratch_shapes=[
            pltpu.VMEM((total_rows, 128), F32),
            pltpu.VMEM((total_rows, 128), F32),
            pltpu.VMEM((1552, 128), F32),
            pltpu.VMEM((1032, 128), F32),
            pltpu.VMEM((1024, 128), F32),
            pltpu.VMEM((1024, 128), F32),
            pltpu.VMEM((2, 192, 128), F32),
            pltpu.VMEM((192, 128), F32),
            pltpu.VMEM((192, 128), F32),
            pltpu.VMEM((64, 128), F32),
            pltpu.VMEM((3, 64, 128), F32),
            pltpu.SemaphoreType.DMA((2,)),
            pltpu.SemaphoreType.DMA((2,)),
            pltpu.SemaphoreType.DMA((2,)),
            pltpu.SemaphoreType.DMA((6,)),
            pltpu.SemaphoreType.DMA((3,)),
        ],
        compiler_params=pltpu.CompilerParams(collective_id=0, has_side_effects=True),
        name="surplus",
    )(levels, velocity, grid_signs, tiled(concentration), tiled(diffusion))
    combined = pl.pallas_call(
        exchange_kernel,
        out_shape=jax.ShapeDtypeStruct((1032, 128), F32),
        in_specs=[vmem, vmem, vmem],
        out_specs=vmem,
        scratch_shapes=[
            pltpu.VMEM((2048, 128), F32),
            pltpu.VMEM((2064, 128), F32),
            pltpu.VMEM((2064, 128), F32),
            pltpu.VMEM((2048, 128), F32),
            pltpu.VMEM((128, 1, 128), I32),
            pltpu.VMEM((128, 1, 128), I32),
            pltpu.VMEM((8, 128), I32),
            pltpu.SMEM((8, 128), I32),
            pltpu.SemaphoreType.DMA,
            pltpu.SemaphoreType.DMA((3,)),
            pltpu.SemaphoreType.DMA((3,)),
        ],
        compiler_params=pltpu.CompilerParams(collective_id=1, has_side_effects=True),
        name="exchange",
    )(surplus, owner_list, slot_list)
    return combined[:1024].reshape(2, COLS, 8, 128).transpose(0, 2, 1, 3).reshape(1, 16, COLS * 128)


def solution(mesh):
    return jax.shard_map(
        body,
        mesh=mesh,
        in_specs=(
            P("grid", "dom", None),
            P("grid", "dom", None),
            P(),
            P("grid", None),
            P("grid"),
            P(("grid", "dom"), None),
            P(("grid", "dom"), None),
        ),
        out_specs=P("grid", "dom", None),
        check_vma=False,
    )
```

profile of v0, /device:TPU:1, one launch (start us, length us, event | category | flops | bytes accessed | tf_op | source)
XLA Modules:
  0.0 82.0 jit_solution(5875128889467800248)
XLA Ops:
  0.7 28.2 %surplus.1.s_ref = f32[1032,128]{1,0:T(8,128)} custom-call(s32[1,3]{1,0:T(1,128)} %lev_ref.1, f32[4]{0:T(128)} %vel_ref.1, s32[1]{0:T(128)S(6)} %copy.8.sign_ref, f32[1024,128]{1,0:T(8,128)} %bitcast.15, f32[1024,128]{1,0:T(8,128)} %bitcast.16), custom_call_target="tpu_custom_call" | custom-call | tf_op jit(solution)/shard_map/surplus/pallas_call | solution.py:537
  28.8 51.3 %exchange.1 = f32[1032,128]{1,0:T(8,128)} custom-call(f32[1032,128]{1,0:T(8,128)} %surplus.1.s_ref, s32[1,128]{1,0:T(1,128)} %own_ref.1, s32[1,128]{1,0:T(1,128)} %slot_ref.1), custom_call_target="tpu_custom_call" | custom-call | tf_op jit(solution)/shard_map/exchange/pallas_call | solution.py:563
  80.1 1.9 %slice.3 = f32[1024,128]{1,0:T(8,128)} slice(f32[1032,128]{1,0:T(8,128)} %exchange.1), slice={[0:1024], [0:128]} | slice | bytes 1048576 | tf_op jit(solution)/shard_map/slice | solution.py:584
where the time goes:
time: 82.2 us; the launch traced here: 82 us
  Pallas kernels  79.4 us (97%)
  local copies, waits for them, and re-layouts  1.87 us (2%)
    pallas_call x1, Pallas kernels, body(): pl.pallas_call(exchange_kernel, out_shape=jax.ShapeDtypeStruct((1032, 128...  51.3 us
    pallas_call x1, Pallas kernels, body(): pl.pallas_call(surplus_kernel, out_shape=jax.ShapeDtypeStruct((1032, 128)...  28.2 us
    slice x1, local copies, waits for them, and re-layouts, body(): combined[:1024].reshape(2, COLS, 8, 128).transpose(0, 2, 1, 3)  1.87 us

commit v1 on v0

v1 whole, which is shorter than its diff:
```python
import jax
import jax.numpy as jnp
from jax import lax
from jax.experimental import pallas as pl
from jax.experimental.pallas import tpu as pltpu
from jax.sharding import PartitionSpec as P

MESH = pl.DeviceIdType.MESH
F32 = jnp.float32
BF16 = jnp.bfloat16
I32 = jnp.int32

COLS = 64
PAD = 8
TILE_HALO = PAD + 2 * COLS


def tile(at):
    return pl.ds(at * 8, 8)


def node_rows(base, node):
    return pl.ds(base + (node // 8) * COLS * 8 + node % 8, COLS, stride=8)


def dot_exact(left, right):
    first = left.astype(BF16)
    rest = left - first.astype(F32)
    second = rest.astype(BF16)
    third = (rest - second.astype(F32)).astype(BF16)
    total = jnp.dot(third, right, preferred_element_type=F32)
    total = total + jnp.dot(second, right, preferred_element_type=F32)
    return total + jnp.dot(first, right, preferred_element_type=F32)


def lane_matrices(l1, l2, sign):
    source = lax.broadcasted_iota(I32, (128, 128), 0)
    target = lax.broadcasted_iota(I32, (128, 128), 1)
    both = l1 + l2
    low = [0, l1, both]
    top = [jnp.minimum(l1, 7), jnp.minimum(both, 7), 7]
    here = jnp.full((128, 128), sign, F32)
    after = jnp.full((128, 128), sign, F32)
    for field in range(3):
        width = jnp.maximum(top[field] - jnp.minimum(low[field], 7), 0)
        mask = jnp.left_shift(1, width) - 1
        shift = jnp.minimum(low[field], 7)
        fro = jnp.right_shift(source, shift) & mask
        to = jnp.right_shift(target, shift) & mask
        bit = to & (-to)
        same = jnp.where(fro == to, 1.0, 0.0)
        near = jnp.where((to != 0) & ((fro == to - bit) | (fro == to + bit)), -0.5, 0.0)
        plain = same + near
        wraps = (to != 0) & (to + bit == mask + 1) & (fro == 0)
        carry = jnp.where(wraps, -0.5, 0.0)
        here = here * plain
        if field == 0:
            after = after * plain
        elif field == 1:
            after = after * jnp.where(both > 6, jnp.where(width > 0, carry, 0.0), plain)
        else:
            after = after * jnp.where(both > 6, 1.0, carry)
    return here, after


def peer_offsets():
    offsets = [(k // 32, k // 8 % 4, k // 2 % 4, k % 2) for k in range(1, 128)]
    return sorted(offsets, key=lambda o: -sum(min(v, 4 - v) for v in o[:3]))


def unrolled(count, factor, step):
    def some(i, carry):
        for k in range(factor):
            step(i * factor + k)
        return carry

    lax.fori_loop(0, count // factor, some, 0)


def combine_kernel(
    lev_ref, vel_ref, sign_ref, own_ref, slot_ref, u_hbm, k_hbm, out_ref,
    start, mid, coef, stepped, lanes_done, rows_done, surplus, packs, low_in, high_in, lead, lead_in,
    out_a, out_b, in_a, in_b, ret_a, ret_b, back_a, back_b, slots_out, slots_in, index_v, index_s,
    load_sem, send_sem, recv_sem, lead_send, lead_recv, slot_sems, out_sems, back_sems,
):
    g = lax.axis_index("grid")
    d = lax.axis_index("dom")
    me = g * 8 + d
    x_at, y_at = lax.div(g, 4), lax.rem(g, 4)
    z_at, core = lax.div(d, 2), lax.rem(d, 2)
    barrier = pltpu.get_barrier_semaphore()

    load_u = pltpu.make_async_copy(u_hbm, start.at[pl.ds(PAD * 8, 1024)], load_sem.at[0])
    load_k = pltpu.make_async_copy(k_hbm, coef.at[pl.ds(0, 1024)], load_sem.at[1])
    load_u.start()
    load_k.start()

    def peer(offset):
        px = lax.rem(x_at + offset[0], 4)
        py = lax.rem(y_at + offset[1], 4)
        pz = lax.rem(z_at + offset[2], 4)
        return px * 4 + py, pz * 2 + lax.rem(core + offset[3], 2)

    offsets = peer_offsets()
    for offset in offsets:
        pl.semaphore_signal(barrier, inc=1, device_id=peer(offset), device_id_type=MESH)

    owners = own_ref[...]
    own_row = jnp.broadcast_to(owners, (128, 128))
    own_col = own_row.T
    row = lax.broadcasted_iota(I32, (128, 128), 0)
    col = lax.broadcasted_iota(I32, (128, 128), 1)
    earlier = jnp.where((own_row == own_col) & (row < col), 1, 0)
    rank = jnp.sum(earlier, axis=0, keepdims=True)
    rank_row = jnp.broadcast_to(rank, (128, 128))
    rank_col = rank_row.T
    slot_row = jnp.broadcast_to(slot_ref[...], (128, 128))
    table = jnp.full((128, 128), -1, I32)
    index_v[...] = jnp.zeros((8, 128), I32)
    index_v[0:1] = 2 * owners + rank
    for r in range(2):
        to_owner = (own_col == col) & (rank_col == r)
        index_v[1 + r : 2 + r] = jnp.sum(jnp.where(to_owner, row, 0), axis=0, keepdims=True)
        of_block = (own_row == row) & (rank_row == r)
        ids = jnp.sum(jnp.where(of_block, slot_row + 1, 0), axis=1, keepdims=True) - 1
        table = jnp.where(col == r, ids, table)
    slots_out[:, 0, :] = table
    fetch = pltpu.make_async_copy(index_v, index_s, load_sem.at[2])
    fetch.start()

    zero_pad = jnp.zeros((PAD * 8, 128), F32)
    for buffer in (start, mid):
        buffer[0 : PAD * 8] = zero_pad
        buffer[(TILE_HALO + COLS) * 8 : (TILE_HALO + COLS + PAD) * 8] = zero_pad
    halo = TILE_HALO * 8
    start[halo : halo + COLS * 8] = jnp.zeros((COLS * 8, 128), F32)
    coef[1024:1536] = jnp.zeros((512, 128), F32)
    stepped[1024:1032] = jnp.zeros((8, 128), F32)

    def halo_rows(s):
        return pl.ds(halo + s, COLS, stride=8)

    def halo_coef(s):
        return pl.ds(1024 + s, COLS, stride=8)

    base = PAD * 8
    load_u.wait()
    load_k.wait()
    packs[0, 0:64] = start[node_rows(base, 0), :]
    packs[0, 64:128] = start[node_rows(base, 1), :]
    packs[0, 128:192] = coef[node_rows(0, 0), :]
    packs[1, 0:64] = start[node_rows(base, 14), :]
    packs[1, 64:128] = start[node_rows(base, 15), :]
    packs[1, 128:192] = coef[node_rows(0, 15), :]
    start[halo_rows(2), :] = packs[0, 0:64]
    start[halo_rows(3), :] = packs[0, 64:128]
    start[halo_rows(4), :] = packs[1, 0:64]
    start[halo_rows(5), :] = packs[1, 64:128]
    coef[halo_coef(2), :] = packs[0, 128:192]
    coef[halo_coef(5), :] = packs[1, 128:192]

    l1 = lev_ref[0, 0]
    l2 = lev_ref[0, 1]
    l3 = lev_ref[0, 2]
    both = l1 + l2
    lane = lax.broadcasted_iota(I32, (8, 128), 1)
    sub = lax.broadcasted_iota(I32, (8, 128), 0)
    span2 = jnp.left_shift(1, l1)
    span3 = jnp.minimum(jnp.left_shift(1, both), 128)
    skip3 = jnp.where(both == 8, 2, jnp.where(both == 9, 4, jnp.where(both == 10, 8, 1)))
    last1 = jnp.left_shift(1, l1) - 1
    last2 = jnp.left_shift(1, l2) - 1
    last3 = jnp.left_shift(1, l3) - 1
    drift1 = 0.1 * vel_ref[0]
    drift2 = 0.1 * vel_ref[1]
    drift3 = 0.1 * vel_ref[2]
    drift4 = 0.1 * vel_ref[3]
    from_next2 = lane < span2
    from_last2 = lane >= 128 - span2
    from_next3 = lane < span3
    from_last3 = lane >= 128 - span3
    ahead2 = (128 - span2) & 127
    behind2 = span2 & 127
    ahead3 = (128 - span3) & 127
    behind3 = span3 & 127

    def masks(c):
        cell = c * 128 + lane
        i1 = cell & last1
        i2 = jnp.right_shift(cell, l1) & last2
        i3 = jnp.right_shift(cell, both) & last3
        return (i1 != last1, i1 != 0, i2 != last2, i2 != 0, i3 != last3, i3 != 0)

    def advance(ref, at, x, ahead4, behind4, diff, ok):
        p1 = jnp.where(ok[0], pltpu.roll(x, 127, 1), 0.0)
        m1 = jnp.where(ok[1], pltpu.roll(x, 1, 1), 0.0)
        p2 = pltpu.roll(jnp.where(from_next2, ref[tile(at + 1), :], x), ahead2, 1)
        p2 = jnp.where(ok[2], p2, 0.0)
        m2 = pltpu.roll(jnp.where(from_last2, ref[tile(at - 1), :], x), behind2, 1)
        m2 = jnp.where(ok[3], m2, 0.0)
        p3 = pltpu.roll(jnp.where(from_next3, ref[tile(at + skip3), :], x), ahead3, 1)
        p3 = jnp.where(ok[4], p3, 0.0)
        m3 = pltpu.roll(jnp.where(from_last3, ref[tile(at - skip3), :], x), behind3, 1)
        m3 = jnp.where(ok[5], m3, 0.0)
        second = ((p1 + m1) + (p2 + m2)) + ((p3 + m3) + (ahead4 + behind4)) - 8.0 * x
        drift = (drift1 * (p1 - m1) + drift2 * (p2 - m2)) + (
            drift3 * (p3 - m3) + drift4 * (ahead4 - behind4)
        )
        return x + 0.1 * diff * second - drift

    def both_groups(ref, c, target, offset, with_halo):
        ok = masks(c)
        x0 = ref[tile(PAD + c), :]
        x1 = ref[tile(PAD + COLS + c), :]
        down0, up1 = x0, x1
        if with_halo:
            xh = ref[tile(TILE_HALO + c), :]
            down0 = jnp.where(sub == 7, pltpu.roll(xh, 6, 0), x0)
            up1 = jnp.where(sub == 0, pltpu.roll(xh, 2, 0), x1)
        value0 = advance(
            ref, PAD + c, x0, pltpu.roll(jnp.where(sub == 0, x1, x0), 7, 0),
            pltpu.roll(down0, 1, 0), coef[tile(c), :], ok,
        )
        value1 = advance(
            ref, PAD + COLS + c, x1, pltpu.roll(up1, 7, 0),
            pltpu.roll(jnp.where(sub == 7, x0, x1), 1, 0), coef[tile(COLS + c), :], ok,
        )
        target[tile(offset + c), :] = value0
        target[tile(offset + COLS + c), :] = value1

    unrolled(COLS, 2, lambda c: both_groups(start, c, mid, PAD, False))

    pl.semaphore_wait(barrier, 127)

    def down():
        return pltpu.make_async_remote_copy(
            src_ref=packs.at[0], dst_ref=high_in, send_sem=send_sem.at[0], recv_sem=recv_sem.at[0],
            device_id=(g, lax.rem(d + 7, 8)), device_id_type=MESH,
        )

    def upward():
        return pltpu.make_async_remote_copy(
            src_ref=packs.at[1], dst_ref=low_in, send_sem=send_sem.at[1], recv_sem=recv_sem.at[1],
            device_id=(g, lax.rem(d + 1, 8)), device_id_type=MESH,
        )

    @pl.when(d > 0)
    def _():
        down().start()

    @pl.when(d < 7)
    def _():
        upward().start()

    def send_all(sources, targets, sems, size):
        for offset in offsets:
            pg, pd = peer(offset)
            pltpu.make_async_remote_copy(
                src_ref=sources.at[pl.ds((pg * 8 + pd) * size, size)],
                dst_ref=targets.at[pl.ds(me * size, size)],
                send_sem=sems.at[0], recv_sem=sems.at[1],
                device_id=(pg, pd), device_id_type=MESH,
            ).start()
        targets[pl.ds(me * size, size)] = sources[pl.ds(me * size, size)]

    def all_of(sources, targets, sems, size):
        return pltpu.make_async_remote_copy(
            src_ref=sources.at[pl.ds(0, 127 * size)], dst_ref=targets.at[pl.ds(0, 127 * size)],
            send_sem=sems.at[0], recv_sem=sems.at[1],
            device_id=(g, lax.rem(d + 1, 8)), device_id_type=MESH,
        )

    send_all(slots_out, slots_in, slot_sems, 1)
    fetch.wait()

    zero_rows = jnp.zeros((192, 128), F32)

    @pl.when(d == 0)
    def _():
        low_in[...] = zero_rows

    @pl.when(d == 7)
    def _():
        high_in[...] = zero_rows

    here, after = lane_matrices(l1, l2, sign_ref[0].astype(F32))
    here = here.astype(BF16)
    after = after.astype(BF16)

    @pl.when(d < 7)
    def _():
        down().wait_recv()

    @pl.when(d > 0)
    def _():
        upward().wait_recv()

    start[halo_rows(0), :] = low_in[0:64]
    start[halo_rows(1), :] = low_in[64:128]
    start[halo_rows(6), :] = high_in[0:64]
    start[halo_rows(7), :] = high_in[64:128]
    coef[halo_coef(1), :] = low_in[128:192]
    coef[halo_coef(6), :] = high_in[128:192]
    outside = jnp.where(d == 0, 1, jnp.where(d == 7, 6, -1))

    def first_halo(c):
        xh = start[tile(TILE_HALO + c), :]
        value = advance(
            start, TILE_HALO + c, xh, pltpu.roll(xh, 7, 0), pltpu.roll(xh, 1, 0),
            coef[tile(2 * COLS + c), :], masks(c),
        )
        mid[tile(TILE_HALO + c), :] = jnp.where(sub == outside, 0.0, value)

    unrolled(COLS, 4, first_halo)
    mid[node_rows(base, 0), :] = mid[halo_rows(2), :]
    mid[node_rows(base, 15), :] = mid[halo_rows(5), :]
    unrolled(COLS, 2, lambda c: both_groups(mid, c, stepped, 0, True))

    straddles = jnp.where(both > 7, jnp.where(l1 < 7, 1, 0), jnp.where(both == 6, 1, 0))
    mask_a = jnp.where(both > 7, skip3 - 1, COLS - 1)
    no_next = jnp.where(straddles == 1, mask_a, 0)
    limit_a = jnp.where(both > 7, span2, span3)
    mask_b = jnp.where(both > 7, COLS - skip3, 0)
    inside = lane < limit_a
    chunk = 128

    def lane_part(i):
        at = i * chunk
        x = stepped[pl.ds(at, chunk), :]
        beyond = stepped[pl.ds(at + 8, chunk), :]
        column = jnp.right_shift(at + lax.broadcasted_iota(I32, (chunk, 128), 0), 3)
        beyond = jnp.where((column & no_next) != no_next, beyond, 0.0)
        lanes_done[pl.ds(at, chunk), :] = dot_exact(x, here) + dot_exact(beyond, after)

    def columns(source, target, t, mask, chosen):
        def step(c):
            j = c & mask
            off = j & (-j)
            has_up = (j != 0) & (j + off <= mask)
            weight = jnp.where(j != 0, 0.5, 0.0)
            weight_up = jnp.where(has_up, 0.5, 0.0)
            at = t * COLS + c
            update = weight * source[tile(at - off), :]
            update = update + weight_up * source[tile(jnp.where(has_up, at + off, at)), :]
            if chosen is not None:
                update = jnp.where(chosen, update, 0.0)
            target[tile(at), :] = source[tile(at), :] - update

        unrolled(COLS, 4, step)

    def lead_copy(slot, target, sent):
        return pltpu.make_async_remote_copy(
            src_ref=lead, dst_ref=lead_in.at[slot], send_sem=lead_send.at[sent],
            recv_sem=lead_recv.at[slot], device_id=(g, target), device_id_type=MESH,
        )

    routes = [(0, d > 0, lax.rem(d + 7, 8)), (1, lax.rem(d, 2) == 0, lax.rem(d + 1, 8))]
    routes += [(1, d == 0, 2), (1, d == 0, 4), (1, d == 4, 6), (2, d == 4, 2)]
    for t in range(2):
        for i in range(512 // chunk):
            lane_part(t * (512 // chunk) + i)
        columns(lanes_done, rows_done, t, mask_a, inside)
        columns(rows_done, lanes_done, t, mask_b, None)
        if t == 0:
            lead[...] = lanes_done[node_rows(0, 0), :]
            for sent, (slot, condition, target) in enumerate(routes):

                @pl.when(condition)
                def _():
                    lead_copy(slot, target, sent).start()

    odd = (sub & 1) == 1
    two = (sub & 3) == 2
    four = sub == 4

    def fourth(c):
        x0 = lanes_done[tile(c), :]
        x1 = lanes_done[tile(COLS + c), :]
        for t, x, y, special in ((0, x0, jnp.where(sub == 0, x1, x0), 0.0), (1, x1, jnp.where(sub == 0, 0.0, x1), x0)):
            near1 = pltpu.roll(y, 7, 0) + pltpu.roll(x, 1, 0)
            near2 = pltpu.roll(y, 6, 0) + pltpu.roll(x, 2, 0)
            near4 = pltpu.roll(y, 4, 0) + pltpu.roll(x, 4, 0)
            near = jnp.where(odd, near1, jnp.where(two, near2, jnp.where(four, near4, special)))
            surplus[tile(t * COLS + c), :] = x - 0.5 * near

    unrolled(COLS, 2, fourth)

    zero_lead = jnp.zeros((64, 128), F32)

    @pl.when(d == 7)
    def _():
        lead_in[0] = zero_lead

    @pl.when(d == 0)
    def _():
        lead_in[1] = zero_lead

    @pl.when(d != 2)
    def _():
        lead_in[2] = zero_lead

    @pl.when(d < 7)
    def _():
        lead_copy(0, lax.rem(d + 7, 8), 0).wait_recv()

    @pl.when(d > 0)
    def _():
        lead_copy(1, lax.rem(d + 1, 8), 0).wait_recv()

    @pl.when(d == 2)
    def _():
        lead_copy(2, lax.rem(d + 1, 8), 0).wait_recv()

    following = 0.5 * lead_in[0]
    use_next = jnp.where(lax.rem(d, 2) == 1, 1.0, 0.0)
    around = 0.5 * (lead_in[1] + lead_in[2]) + use_next * following
    surplus[node_rows(0, 0), :] = surplus[node_rows(0, 0), :] - around
    for node in (8, 12, 14, 15):
        surplus[node_rows(0, node), :] = surplus[node_rows(0, node), :] - following

    def block_rows(block, half):
        node = lax.div(block, 8)
        at = (lax.div(node, 8) * COLS + lax.rem(block, 8) * 8) * 8 + lax.rem(node, 8)
        return pl.ds(at + half * 32, 4, stride=8)

    def pack(half, target):
        def step(o):
            for r in range(2):
                target[pl.ds(o * 8 + r * 4, 4), :] = surplus[block_rows(index_s[1 + r, o], half), :]

        unrolled(128, 4, step)

    halves = ((out_a, in_a, ret_a, back_a), (out_b, in_b, ret_b, back_b))
    for half, (outgoing, arrived, _, _) in enumerate(halves):
        pack(half, outgoing)
        send_all(outgoing, arrived, out_sems.at[half], 8)

    all_of(slots_out, slots_in, slot_sems, 1).wait_recv()
    ids_col = slots_in[:, 0, :]
    ids_row = ids_col.T
    equal = []
    for r in range(2):
        of_r = jnp.broadcast_to(ids_col[:, r : r + 1], (128, 128))
        parts = [
            jnp.where(of_r == jnp.broadcast_to(ids_row[s : s + 1, :], (128, 128)), 1.0, 0.0)
            for s in range(2)
        ]
        equal.append(jnp.concatenate(parts, axis=1))
    equal = jnp.concatenate(equal, axis=0).astype(BF16)

    for half, (outgoing, arrived, returned, back) in enumerate(halves):
        all_of(outgoing, arrived, out_sems.at[half], 8).wait_recv()
        for j in range(4):
            block = jnp.concatenate(
                [arrived[pl.ds(r * 4 + j, 128, stride=8), :] for r in range(2)], axis=0
            )
            first = block.astype(BF16)
            rest = block - first.astype(F32)
            second = rest.astype(BF16)
            third = (rest - second.astype(F32)).astype(BF16)
            total = jnp.dot(equal, third, preferred_element_type=F32)
            total = total + jnp.dot(equal, second, preferred_element_type=F32)
            total = total + jnp.dot(equal, first, preferred_element_type=F32)
            for r in range(2):
                returned[pl.ds(r * 4 + j, 128, stride=8), :] = total[r * 128 : (r + 1) * 128]
        send_all(returned, back, back_sems.at[half], 8)

    for half, (_, _, returned, back) in enumerate(halves):
        all_of(returned, back, back_sems.at[half], 8).wait_recv()

        def unpack(b):
            out_ref[block_rows(b, half), :] = back[pl.ds(index_s[0, b] * 4, 4), :]

        unrolled(128, 4, unpack)

    @pl.when(d > 0)
    def _():
        down().wait_send()

    @pl.when(d < 7)
    def _():
        upward().wait_send()

    for sent, (slot, condition, target) in enumerate(routes):

        @pl.when(condition)
        def _():
            lead_copy(slot, target, sent).wait_send()

    all_of(slots_out, slots_in, slot_sems, 1).wait_send()
    for half, (outgoing, arrived, returned, back) in enumerate(halves):
        all_of(outgoing, arrived, out_sems.at[half], 8).wait_send()
        all_of(returned, back, back_sems.at[half], 8).wait_send()


def body(concentration, diffusion, velocity, levels, grid_signs, owner_list, slot_list):
    def tiled(block):
        return block.reshape(2, 8, COLS, 128).transpose(0, 2, 1, 3).reshape(1024, 128)

    smem = pl.BlockSpec(memory_space=pltpu.SMEM)
    vmem = pl.BlockSpec(memory_space=pltpu.VMEM)
    anywhere = pl.BlockSpec(memory_space=pl.ANY)
    total_rows = (TILE_HALO + COLS + PAD) * 8
    rows = [total_rows, total_rows, 1552, 1032, 1032, 1032, 1032]
    combined = pl.pallas_call(
        combine_kernel,
        out_shape=jax.ShapeDtypeStruct((1032, 128), F32),
        in_specs=[smem, smem, smem, vmem, vmem, anywhere, anywhere],
        out_specs=vmem,
        scratch_shapes=[pltpu.VMEM((n, 128), F32) for n in rows]
        + [
            pltpu.VMEM((2, 192, 128), F32),
            pltpu.VMEM((192, 128), F32),
            pltpu.VMEM((192, 128), F32),
            pltpu.VMEM((64, 128), F32),
            pltpu.VMEM((3, 64, 128), F32),
        ]
        + [pltpu.VMEM((1032, 128), F32) for _ in range(8)]
        + [
            pltpu.VMEM((128, 1, 128), I32),
            pltpu.VMEM((128, 1, 128), I32),
            pltpu.VMEM((8, 128), I32),
            pltpu.SMEM((8, 128), I32),
            pltpu.SemaphoreType.DMA((3,)),
            pltpu.SemaphoreType.DMA((2,)),
            pltpu.SemaphoreType.DMA((2,)),
            pltpu.SemaphoreType.DMA((6,)),
            pltpu.SemaphoreType.DMA((3,)),
            pltpu.SemaphoreType.DMA((2,)),
            pltpu.SemaphoreType.DMA((2, 2)),
            pltpu.SemaphoreType.DMA((2, 2)),
        ],
        compiler_params=pltpu.CompilerParams(collective_id=0, has_side_effects=True),
        name="combine",
    )(levels, velocity, grid_signs, owner_list, slot_list, tiled(concentration), tiled(diffusion))
    return combined[:1024].reshape(2, COLS, 8, 128).transpose(0, 2, 1, 3).reshape(1, 16, COLS * 128)


def solution(mesh):
    return jax.shard_map(
        body,
        mesh=mesh,
        in_specs=(
            P("grid", "dom", None),
            P("grid", "dom", None),
            P(),
            P("grid", None),
            P("grid"),
            P(("grid", "dom"), None),
            P(("grid", "dom"), None),
        ),
        out_specs=P("grid", "dom", None),
        check_vma=False,
    )
```

time: 82.2 us -> 56.7 us (0.69)
  Pallas kernels: 79.4 us -> 53.4 us
    pallas_call x2 -> x1, Pallas kernels: 79.4 us -> 53.4 us  [body(): pl.pallas_call(combine_kernel, out_shape=jax.ShapeDtypeStruct((1032, 128)...]
where the time goes in v1:
time: 56.7 us; the launch traced here: 55.9 us
  Pallas kernels  53.4 us (94%)
  local copies, waits for them, and re-layouts  1.87 us (3%)
  between operations  0.66 us (1%)
    pallas_call x1, Pallas kernels, body(): pl.pallas_call(combine_kernel, out_shape=jax.ShapeDtypeStruct((1032, 128)...  53.4 us
    slice x1, local copies, waits for them, and re-layouts, body(): combined[:1024].reshape(2, COLS, 8, 128).transpose(0, 2, 1, 3)  1.87 us

profile of v1, /device:TPU:1, one launch (start us, length us, event | category | flops | bytes accessed | tf_op | source)
XLA Modules:
  0.0 55.9 jit_solution(9205334484471719987)
XLA Ops:
  0.7 53.4 %combine.1 = f32[1032,128]{1,0:T(8,128)} custom-call(s32[1,3]{1,0:T(1,128)} %lev_ref.1, f32[4]{0:T(128)} %vel_ref.1, s32[1]{0:T(128)S(6)} %copy.8.sign_ref, s32[1,128]{1,0:T(1,128)} %own_ref.1, s32[1,128]{1,0:T(1,128)} %slot_ref.1, f32[1024,128]{1,0:T(8,128)} %bitcast.15, f32[1024,128]{1,0:T(8,128)} %bitcast.16), custom_call_target="tpu_custom_call" | custom-call | tf_op jit(solution)/shard_map/combine/pallas_call | solution.py:505
  54.0 1.9 %slice.3 = f32[1024,128]{1,0:T(8,128)} slice(f32[1032,128]{1,0:T(8,128)} %combine.1), slice={[0:1024], [0:128]} | slice | bytes 1048576 | tf_op jit(solution)/shard_map/slice | solution.py:536

commit v2 on v1

--- a/solution.py
+++ b/solution.py
@@ -23,13 +23,10 @@
     return pl.ds(base + (node // 8) * COLS * 8 + node % 8, COLS, stride=8)
 
 
-def dot_exact(left, right):
+def dot_split(left, right):
     first = left.astype(BF16)
-    rest = left - first.astype(F32)
-    second = rest.astype(BF16)
-    third = (rest - second.astype(F32)).astype(BF16)
-    total = jnp.dot(third, right, preferred_element_type=F32)
-    total = total + jnp.dot(second, right, preferred_element_type=F32)
+    second = (left - first.astype(F32)).astype(BF16)
+    total = jnp.dot(second, right, preferred_element_type=F32)
     return total + jnp.dot(first, right, preferred_element_type=F32)
 
 
@@ -86,8 +83,10 @@
     g = lax.axis_index("grid")
     d = lax.axis_index("dom")
     me = g * 8 + d
-    x_at, y_at = lax.div(g, 4), lax.rem(g, 4)
-    z_at, core = lax.div(d, 2), lax.rem(d, 2)
+    x_at, y_at = g // 4, g % 4
+    z_at, core = d // 2, d % 2
+    grids = [((x_at + i) % 4) * 4 + (y_at + j) % 4 for i in range(4) for j in range(4)]
+    doms = [((z_at + i) % 4) * 2 + (core + j) % 2 for i in range(4) for j in range(2)]
     barrier = pltpu.get_barrier_semaphore()
 
     load_u = pltpu.make_async_copy(u_hbm, start.at[pl.ds(PAD * 8, 1024)], load_sem.at[0])
@@ -96,10 +95,7 @@
     load_k.start()
 
     def peer(offset):
-        px = lax.rem(x_at + offset[0], 4)
-        py = lax.rem(y_at + offset[1], 4)
-        pz = lax.rem(z_at + offset[2], 4)
-        return px * 4 + py, pz * 2 + lax.rem(core + offset[3], 2)
+        return grids[offset[0] * 4 + offset[1]], doms[offset[2] * 2 + offset[3]]
 
     offsets = peer_offsets()
     for offset in offsets:
@@ -117,10 +113,15 @@
     slot_row = jnp.broadcast_to(slot_ref[...], (128, 128))
     table = jnp.full((128, 128), -1, I32)
     index_v[...] = jnp.zeros((8, 128), I32)
-    index_v[0:1] = 2 * owners + rank
+    second_one = jnp.minimum(rank, 1)
+    index_v[0:1] = 8 * owners + 4 * second_one
+    index_v[3:4] = 8 * owners + 4 * (1 - second_one)
+    first_row = (row // 64) * (8 * COLS) + (row % 8) * 64 + (row // 8) % 8
     for r in range(2):
         to_owner = (own_col == col) & (rank_col == r)
-        index_v[1 + r : 2 + r] = jnp.sum(jnp.where(to_owner, row, 0), axis=0, keepdims=True)
+        index_v[1 + r : 2 + r] = jnp.sum(
+            jnp.where(to_owner, first_row, 0), axis=0, keepdims=True
+        )
         of_block = (own_row == row) & (rank_row == r)
         ids = jnp.sum(jnp.where(of_block, slot_row + 1, 0), axis=1, keepdims=True) - 1
         table = jnp.where(col == r, ids, table)
@@ -128,14 +129,9 @@
     fetch = pltpu.make_async_copy(index_v, index_s, load_sem.at[2])
     fetch.start()
 
-    zero_pad = jnp.zeros((PAD * 8, 128), F32)
-    for buffer in (start, mid):
-        buffer[0 : PAD * 8] = zero_pad
-        buffer[(TILE_HALO + COLS) * 8 : (TILE_HALO + COLS + PAD) * 8] = zero_pad
+    lanes_done[1024:1032] = jnp.zeros((8, 128), F32)
+    rows_done[1024:1032] = jnp.zeros((8, 128), F32)
     halo = TILE_HALO * 8
-    start[halo : halo + COLS * 8] = jnp.zeros((COLS * 8, 128), F32)
-    coef[1024:1536] = jnp.zeros((512, 128), F32)
-    stepped[1024:1032] = jnp.zeros((8, 128), F32)
 
     def halo_rows(s):
         return pl.ds(halo + s, COLS, stride=8)
@@ -184,12 +180,15 @@
     ahead3 = (128 - span3) & 127
     behind3 = span3 & 127
 
+    i1 = lane & last1
+    not_last1 = i1 != last1
+    not_first1 = i1 != 0
+
     def masks(c):
         cell = c * 128 + lane
-        i1 = cell & last1
         i2 = jnp.right_shift(cell, l1) & last2
         i3 = jnp.right_shift(cell, both) & last3
-        return (i1 != last1, i1 != 0, i2 != last2, i2 != 0, i3 != last3, i3 != 0)
+        return (not_last1, not_first1, i2 != last2, i2 != 0, i3 != last3, i3 != 0)
 
     def advance(ref, at, x, ahead4, behind4, diff, ok):
         p1 = jnp.where(ok[0], pltpu.roll(x, 127, 1), 0.0)
@@ -330,21 +329,22 @@
         beyond = stepped[pl.ds(at + 8, chunk), :]
         column = jnp.right_shift(at + lax.broadcasted_iota(I32, (chunk, 128), 0), 3)
         beyond = jnp.where((column & no_next) != no_next, beyond, 0.0)
-        lanes_done[pl.ds(at, chunk), :] = dot_exact(x, here) + dot_exact(beyond, after)
-
-    def columns(source, target, t, mask, chosen):
+        lanes_done[pl.ds(at, chunk), :] = dot_split(x, here) + dot_split(beyond, after)
+
+    nothing = 2 * COLS
+
+    def columns(source, target, mask, chosen):
         def step(c):
             j = c & mask
             off = j & (-j)
             has_up = (j != 0) & (j + off <= mask)
-            weight = jnp.where(j != 0, 0.5, 0.0)
-            weight_up = jnp.where(has_up, 0.5, 0.0)
-            at = t * COLS + c
-            update = weight * source[tile(at - off), :]
-            update = update + weight_up * source[tile(jnp.where(has_up, at + off, at)), :]
-            if chosen is not None:
-                update = jnp.where(chosen, update, 0.0)
-            target[tile(at), :] = source[tile(at), :] - update
+            for t in range(2):
+                lower = jnp.where(j != 0, t * COLS + c - off, nothing)
+                upper = jnp.where(has_up, t * COLS + c + off, nothing)
+                update = 0.5 * (source[tile(lower), :] + source[tile(upper), :])
+                if chosen is not None:
+                    update = jnp.where(chosen, update, 0.0)
+                target[tile(t * COLS + c), :] = source[tile(t * COLS + c), :] - update
 
         unrolled(COLS, 4, step)
 
@@ -356,18 +356,16 @@
 
     routes = [(0, d > 0, lax.rem(d + 7, 8)), (1, lax.rem(d, 2) == 0, lax.rem(d + 1, 8))]
     routes += [(1, d == 0, 2), (1, d == 0, 4), (1, d == 4, 6), (2, d == 4, 2)]
-    for t in range(2):
-        for i in range(512 // chunk):
-            lane_part(t * (512 // chunk) + i)
-        columns(lanes_done, rows_done, t, mask_a, inside)
-        columns(rows_done, lanes_done, t, mask_b, None)
-        if t == 0:
-            lead[...] = lanes_done[node_rows(0, 0), :]
-            for sent, (slot, condition, target) in enumerate(routes):
-
-                @pl.when(condition)
-                def _():
-                    lead_copy(slot, target, sent).start()
+    for i in range(1024 // chunk):
+        lane_part(i)
+    columns(lanes_done, rows_done, mask_a, inside)
+    columns(rows_done, lanes_done, mask_b, None)
+    lead[...] = lanes_done[node_rows(0, 0), :]
+    for sent, (slot, condition, target) in enumerate(routes):
+
+        @pl.when(condition)
+        def _():
+            lead_copy(slot, target, sent).start()
 
     odd = (sub & 1) == 1
     two = (sub & 3) == 2
@@ -384,56 +382,6 @@
             surplus[tile(t * COLS + c), :] = x - 0.5 * near
 
     unrolled(COLS, 2, fourth)
-
-    zero_lead = jnp.zeros((64, 128), F32)
-
-    @pl.when(d == 7)
-    def _():
-        lead_in[0] = zero_lead
-
-    @pl.when(d == 0)
-    def _():
-        lead_in[1] = zero_lead
-
-    @pl.when(d != 2)
-    def _():
-        lead_in[2] = zero_lead
-
-    @pl.when(d < 7)
-    def _():
-        lead_copy(0, lax.rem(d + 7, 8), 0).wait_recv()
-
-    @pl.when(d > 0)
-    def _():
-        lead_copy(1, lax.rem(d + 1, 8), 0).wait_recv()
-
-    @pl.when(d == 2)
-    def _():
-        lead_copy(2, lax.rem(d + 1, 8), 0).wait_recv()
-
-    following = 0.5 * lead_in[0]
-    use_next = jnp.where(lax.rem(d, 2) == 1, 1.0, 0.0)
-    around = 0.5 * (lead_in[1] + lead_in[2]) + use_next * following
-    surplus[node_rows(0, 0), :] = surplus[node_rows(0, 0), :] - around
-    for node in (8, 12, 14, 15):
-        surplus[node_rows(0, node), :] = surplus[node_rows(0, node), :] - following
-
-    def block_rows(block, half):
-        node = lax.div(block, 8)
-        at = (lax.div(node, 8) * COLS + lax.rem(block, 8) * 8) * 8 + lax.rem(node, 8)
-        return pl.ds(at + half * 32, 4, stride=8)
-
-    def pack(half, target):
-        def step(o):
-            for r in range(2):
-                target[pl.ds(o * 8 + r * 4, 4), :] = surplus[block_rows(index_s[1 + r, o], half), :]
-
-        unrolled(128, 4, step)
-
-    halves = ((out_a, in_a, ret_a, back_a), (out_b, in_b, ret_b, back_b))
-    for half, (outgoing, arrived, _, _) in enumerate(halves):
-        pack(half, outgoing)
-        send_all(outgoing, arrived, out_sems.at[half], 8)
 
     all_of(slots_out, slots_in, slot_sems, 1).wait_recv()
     ids_col = slots_in[:, 0, :]
@@ -448,30 +396,71 @@
         equal.append(jnp.concatenate(parts, axis=1))
     equal = jnp.concatenate(equal, axis=0).astype(BF16)
 
+    zero_lead = jnp.zeros((64, 128), F32)
+
+    @pl.when(d == 7)
+    def _():
+        lead_in[0] = zero_lead
+
+    @pl.when(d == 0)
+    def _():
+        lead_in[1] = zero_lead
+
+    @pl.when(d != 2)
+    def _():
+        lead_in[2] = zero_lead
+
+    @pl.when(d < 7)
+    def _():
+        lead_copy(0, lax.rem(d + 7, 8), 0).wait_recv()
+
+    @pl.when(d > 0)
+    def _():
+        lead_copy(1, lax.rem(d + 1, 8), 0).wait_recv()
+
+    @pl.when(d == 2)
+    def _():
+        lead_copy(2, lax.rem(d + 1, 8), 0).wait_recv()
+
+    following = 0.5 * lead_in[0]
+    use_next = jnp.where(lax.rem(d, 2) == 1, 1.0, 0.0)
+    around = 0.5 * (lead_in[1] + lead_in[2]) + use_next * following
+    surplus[node_rows(0, 0), :] = surplus[node_rows(0, 0), :] - around
+    for node in (8, 12, 14, 15):
+        surplus[node_rows(0, node), :] = surplus[node_rows(0, node), :] - following
+
+    for o in range(128):
+        of_rank = [surplus[pl.ds(index_s[1 + r, o], 8, stride=8), :] for r in range(2)]
+        turned = pltpu.roll(of_rank[1], 4, 0)
+        out_a[o * 8 : o * 8 + 8, :] = jnp.where(sub < 4, of_rank[0], turned)
+        out_b[o * 8 : o * 8 + 8, :] = jnp.where(sub < 4, turned, of_rank[0])
+
+    halves = ((out_a, in_a, ret_a, back_a), (out_b, in_b, ret_b, back_b))
+    for half, (outgoing, arrived, _, _) in enumerate(halves):
+        send_all(outgoing, arrived, out_sems.at[half], 8)
+
     for half, (outgoing, arrived, returned, back) in enumerate(halves):
         all_of(outgoing, arrived, out_sems.at[half], 8).wait_recv()
         for j in range(4):
             block = jnp.concatenate(
-                [arrived[pl.ds(r * 4 + j, 128, stride=8), :] for r in range(2)], axis=0
+                [arrived[pl.ds((r ^ half) * 4 + j, 128, stride=8), :] for r in range(2)], axis=0
             )
             first = block.astype(BF16)
-            rest = block - first.astype(F32)
-            second = rest.astype(BF16)
-            third = (rest - second.astype(F32)).astype(BF16)
-            total = jnp.dot(equal, third, preferred_element_type=F32)
-            total = total + jnp.dot(equal, second, preferred_element_type=F32)
+            second = (block - first.astype(F32)).astype(BF16)
+            total = jnp.dot(equal, second, preferred_element_type=F32)
             total = total + jnp.dot(equal, first, preferred_element_type=F32)
             for r in range(2):
-                returned[pl.ds(r * 4 + j, 128, stride=8), :] = total[r * 128 : (r + 1) * 128]
+                returned[pl.ds((r ^ half) * 4 + j, 128, stride=8), :] = total[
+                    r * 128 : (r + 1) * 128
+                ]
         send_all(returned, back, back_sems.at[half], 8)
 
     for half, (_, _, returned, back) in enumerate(halves):
         all_of(returned, back, back_sems.at[half], 8).wait_recv()
 
-        def unpack(b):
-            out_ref[block_rows(b, half), :] = back[pl.ds(index_s[0, b] * 4, 4), :]
-
-        unrolled(128, 4, unpack)
+        for block in range(128):
+            at = (block // 64) * (8 * COLS) + (block % 8) * 64 + (block // 8) % 8 + half * 32
+            out_ref[pl.ds(at, 4, stride=8), :] = back[pl.ds(index_s[3 * half, block], 4), :]
 
     @pl.when(d > 0)
     def _():
@@ -494,12 +483,16 @@
 
 
 def body(concentration, diffusion, velocity, levels, grid_signs, owner_list, slot_list):
+    def in_hbm(array):
+        return pltpu.with_memory_space_constraint(array, pltpu.HBM)
+
     def tiled(block):
-        return block.reshape(2, 8, COLS, 128).transpose(0, 2, 1, 3).reshape(1024, 128)
+        rows = block.reshape(2, 8, COLS, 128).transpose(0, 2, 1, 3).reshape(1024, 128)
+        return in_hbm(rows)
 
     smem = pl.BlockSpec(memory_space=pltpu.SMEM)
     vmem = pl.BlockSpec(memory_space=pltpu.VMEM)
-    anywhere = pl.BlockSpec(memory_space=pl.ANY)
+    anywhere = pl.BlockSpec(memory_space=pltpu.HBM)
     total_rows = (TILE_HALO + COLS + PAD) * 8
     rows = [total_rows, total_rows, 1552, 1032, 1032, 1032, 1032]
     combined = pl.pallas_call(
@@ -530,9 +523,14 @@
             pltpu.SemaphoreType.DMA((2, 2)),
             pltpu.SemaphoreType.DMA((2, 2)),
         ],
-        compiler_params=pltpu.CompilerParams(collective_id=0, has_side_effects=True),
+        compiler_params=pltpu.CompilerParams(
+            collective_id=0, has_side_effects=True, vmem_limit_bytes=24 << 20
+        ),
         name="combine",
-    )(levels, velocity, grid_signs, owner_list, slot_list, tiled(concentration), tiled(diffusion))
+    )(
+        in_hbm(levels), in_hbm(velocity), grid_signs, in_hbm(owner_list), in_hbm(slot_list),
+        tiled(concentration), tiled(diffusion),
+    )
     return combined[:1024].reshape(2, COLS, 8, 128).transpose(0, 2, 1, 3).reshape(1, 16, COLS * 128)
 
 

time: 56.7 us -> 52.6 us (0.928)
  Pallas kernels: 53.4 us -> 50.9 us
  local copies, waits for them, and re-layouts: 1.87 us -> 0.83 us
    pallas_call x1, Pallas kernels: 53.4 us -> 50.9 us  [body(): pl.pallas_call(combine_kernel, out_shape=jax.ShapeDtypeStruct((1032, 128)...]
    slice x1, local copies, waits for them, and re-layouts: 1.87 us -> 0.83 us  [body(): combined[:1024].reshape(2, COLS, 8, 128).transpose(0, 2, 1, 3)]
where the time goes in v2:
time: 52.6 us; the launch traced here: 52.3 us
  Pallas kernels  50.9 us (97%)
  local copies, waits for them, and re-layouts  0.83 us (2%)
  between operations  0.66 us (1%)
    pallas_call x1, Pallas kernels, body(): pl.pallas_call(combine_kernel, out_shape=jax.ShapeDtypeStruct((1032, 128)...  50.9 us

profile of v2, /device:TPU:1, one launch (start us, length us, event | category | flops | bytes accessed | tf_op | source)
XLA Modules:
  0.0 52.3 jit_solution(6312549931325271383)
XLA Ops:
  0.7 50.9 %combine.1 = f32[1032,128]{1,0:T(8,128)S(1)} custom-call(s32[1,3]{1,0:T(1,128)} %lev_ref.1, f32[4]{0:T(128)} %vel_ref.1, s32[1]{0:T(128)S(6)} %copy.8.sign_ref, s32[1,128]{1,0:T(1,128)} %own_ref.1, s32[1,128]{1,0:T(1,128)} %slot_ref.1, f32[1024,128]{1,0:T(8,128)} %bitcast.15, f32[1024,128]{1,0:T(8,128)} %bitcast.16), custom_call_target="tpu_custom_call" | custom-call | tf_op jit(solution)/shard_map/combine/pallas_call | solution.py:498
  51.5 0.8 %slice.3 = f32[1024,128]{1,0:T(8,128)} slice(f32[1032,128]{1,0:T(8,128)S(1)} %combine.1), slice={[0:1024], [0:128]} | slice | bytes 1048576 | tf_op jit(solution)/shard_map/slice | solution.py:534

commit v3 on v2

--- a/solution.py
+++ b/solution.py
@@ -77,6 +77,7 @@
 def combine_kernel(
     lev_ref, vel_ref, sign_ref, own_ref, slot_ref, u_hbm, k_hbm, out_ref,
     start, mid, coef, stepped, lanes_done, rows_done, surplus, packs, low_in, high_in, lead, lead_in,
+    sums, diffs, forth, back2, turned3,
     out_a, out_b, in_a, in_b, ret_a, ret_b, back_a, back_b, slots_out, slots_in, index_v, index_s,
     load_sem, send_sem, recv_sem, lead_send, lead_recv, slot_sems, out_sems, back_sems,
 ):
@@ -171,38 +172,57 @@
     drift2 = 0.1 * vel_ref[1]
     drift3 = 0.1 * vel_ref[2]
     drift4 = 0.1 * vel_ref[3]
-    from_next2 = lane < span2
-    from_last2 = lane >= 128 - span2
-    from_next3 = lane < span3
-    from_last3 = lane >= 128 - span3
-    ahead2 = (128 - span2) & 127
-    behind2 = span2 & 127
-    ahead3 = (128 - span3) & 127
-    behind3 = span3 & 127
-
-    i1 = lane & last1
-    not_last1 = i1 != last1
-    not_first1 = i1 != 0
+    stays2 = lane < 128 - span2
+    comes2 = lane >= span2
+    stays3 = lane < 128 - span3
+    comes3 = lane >= span3
+
+    source = lax.broadcasted_iota(I32, (128, 128), 0)
+    target = lax.broadcasted_iota(I32, (128, 128), 1)
+    at1 = target & last1
+    from_up = jnp.where((source == target + 1) & (at1 != last1), 1.0, 0.0)
+    from_down = jnp.where((source == target - 1) & (at1 != 0), 1.0, 0.0)
+    turn2 = span2 & 127
+    turn3 = span3 & 127
+    forms = [
+        from_up + from_down,
+        from_up - from_down,
+        jnp.where(source == ((target + turn2) & 127), 1.0, 0.0),
+        jnp.where(source == ((target - turn2) & 127), 1.0, 0.0),
+        jnp.where(source == ((target + turn3) & 127), 1.0, 0.0),
+    ]
+    forms = jnp.concatenate([jnp.concatenate([form, form], axis=0).astype(BF16) for form in forms], axis=1)
+    shift_chunk = 128
+
+    def shift_lanes(ref, at):
+        x = ref[at : at + shift_chunk, :]
+        high = x.astype(BF16)
+        low = (x - high.astype(F32)).astype(BF16)
+        shifted = jnp.dot(
+            jnp.concatenate([high, low], axis=1), forms, preferred_element_type=F32
+        )
+        for form, scratch in enumerate((sums, diffs, forth, back2, turned3)):
+            scratch[at : at + shift_chunk, :] = shifted[:, form * 128 : (form + 1) * 128]
 
     def masks(c):
         cell = c * 128 + lane
         i2 = jnp.right_shift(cell, l1) & last2
         i3 = jnp.right_shift(cell, both) & last3
-        return (not_last1, not_first1, i2 != last2, i2 != 0, i3 != last3, i3 != 0)
-
-    def advance(ref, at, x, ahead4, behind4, diff, ok):
-        p1 = jnp.where(ok[0], pltpu.roll(x, 127, 1), 0.0)
-        m1 = jnp.where(ok[1], pltpu.roll(x, 1, 1), 0.0)
-        p2 = pltpu.roll(jnp.where(from_next2, ref[tile(at + 1), :], x), ahead2, 1)
-        p2 = jnp.where(ok[2], p2, 0.0)
-        m2 = pltpu.roll(jnp.where(from_last2, ref[tile(at - 1), :], x), behind2, 1)
-        m2 = jnp.where(ok[3], m2, 0.0)
-        p3 = pltpu.roll(jnp.where(from_next3, ref[tile(at + skip3), :], x), ahead3, 1)
-        p3 = jnp.where(ok[4], p3, 0.0)
-        m3 = pltpu.roll(jnp.where(from_last3, ref[tile(at - skip3), :], x), behind3, 1)
-        m3 = jnp.where(ok[5], m3, 0.0)
-        second = ((p1 + m1) + (p2 + m2)) + ((p3 + m3) + (ahead4 + behind4)) - 8.0 * x
-        drift = (drift1 * (p1 - m1) + drift2 * (p2 - m2)) + (
+        return (i2 != last2, i2 != 0, i3 != last3, i3 != 0)
+
+    def advance(at, x, ahead4, behind4, diff, ok):
+        here = tile(at)
+        p2 = jnp.where(stays2, forth[here, :], forth[tile(at + 1), :])
+        p2 = jnp.where(ok[0], p2, 0.0)
+        m2 = jnp.where(comes2, back2[here, :], back2[tile(at - 1), :])
+        m2 = jnp.where(ok[1], m2, 0.0)
+        half = turned3[here, :]
+        p3 = jnp.where(stays3, half, turned3[tile(at + skip3), :])
+        p3 = jnp.where(ok[2], p3, 0.0)
+        m3 = jnp.where(comes3, half, turned3[tile(at - skip3), :])
+        m3 = jnp.where(ok[3], m3, 0.0)
+        second = (sums[here, :] + (p2 + m2)) + ((p3 + m3) + (ahead4 + behind4)) - 8.0 * x
+        drift = (drift1 * diffs[here, :] + drift2 * (p2 - m2)) + (
             drift3 * (p3 - m3) + drift4 * (ahead4 - behind4)
         )
         return x + 0.1 * diff * second - drift
@@ -217,16 +237,18 @@
             down0 = jnp.where(sub == 7, pltpu.roll(xh, 6, 0), x0)
             up1 = jnp.where(sub == 0, pltpu.roll(xh, 2, 0), x1)
         value0 = advance(
-            ref, PAD + c, x0, pltpu.roll(jnp.where(sub == 0, x1, x0), 7, 0),
+            PAD + c, x0, pltpu.roll(jnp.where(sub == 0, x1, x0), 7, 0),
             pltpu.roll(down0, 1, 0), coef[tile(c), :], ok,
         )
         value1 = advance(
-            ref, PAD + COLS + c, x1, pltpu.roll(up1, 7, 0),
+            PAD + COLS + c, x1, pltpu.roll(up1, 7, 0),
             pltpu.roll(jnp.where(sub == 7, x0, x1), 1, 0), coef[tile(COLS + c), :], ok,
         )
         target[tile(offset + c), :] = value0
         target[tile(offset + COLS + c), :] = value1
 
+    for i in range(1024 // shift_chunk):
+        shift_lanes(start, PAD * 8 + i * shift_chunk)
     unrolled(COLS, 2, lambda c: both_groups(start, c, mid, PAD, False))
 
     pl.semaphore_wait(barrier, 127)
@@ -305,14 +327,18 @@
     def first_halo(c):
         xh = start[tile(TILE_HALO + c), :]
         value = advance(
-            start, TILE_HALO + c, xh, pltpu.roll(xh, 7, 0), pltpu.roll(xh, 1, 0),
+            TILE_HALO + c, xh, pltpu.roll(xh, 7, 0), pltpu.roll(xh, 1, 0),
             coef[tile(2 * COLS + c), :], masks(c),
         )
         mid[tile(TILE_HALO + c), :] = jnp.where(sub == outside, 0.0, value)
 
+    for i in range(512 // shift_chunk):
+        shift_lanes(start, halo + i * shift_chunk)
     unrolled(COLS, 4, first_halo)
     mid[node_rows(base, 0), :] = mid[halo_rows(2), :]
     mid[node_rows(base, 15), :] = mid[halo_rows(5), :]
+    for i in range(1024 // shift_chunk):
+        shift_lanes(mid, PAD * 8 + i * shift_chunk)
     unrolled(COLS, 2, lambda c: both_groups(mid, c, stepped, 0, True))
 
     straddles = jnp.where(both > 7, jnp.where(l1 < 7, 1, 0), jnp.where(both == 6, 1, 0))
@@ -508,6 +534,7 @@
             pltpu.VMEM((64, 128), F32),
             pltpu.VMEM((3, 64, 128), F32),
         ]
+        + [pltpu.VMEM((total_rows, 128), F32) for _ in range(5)]
         + [pltpu.VMEM((1032, 128), F32) for _ in range(8)]
         + [
             pltpu.VMEM((128, 1, 128), I32),

time: 52.6 us -> 50.4 us (0.958)
  Pallas kernels: 50.9 us -> 48.8 us
    pallas_call x1, Pallas kernels: 50.9 us -> 48.8 us  [body(): pl.pallas_call(combine_kernel, out_shape=jax.ShapeDtypeStruct((1032, 128)...]
where the time goes in v3:
time: 50.4 us; the launch traced here: 50.2 us
  Pallas kernels  48.8 us (97%)
  local copies, waits for them, and re-layouts  0.83 us (2%)
  between operations  0.66 us (1%)
    pallas_call x1, Pallas kernels, body(): pl.pallas_call(combine_kernel, out_shape=jax.ShapeDtypeStruct((1032, 128)...  48.8 us

profile of v3, /device:TPU:1, one launch (start us, length us, event | category | flops | bytes accessed | tf_op | source)
XLA Modules:
  0.0 50.2 jit_solution(16158596740817601331)
XLA Ops:
  0.7 48.8 %combine.1 = f32[1032,128]{1,0:T(8,128)S(1)} custom-call(s32[1,3]{1,0:T(1,128)} %lev_ref.1, f32[4]{0:T(128)} %vel_ref.1, s32[1]{0:T(128)S(6)} %copy.8.sign_ref, s32[1,128]{1,0:T(1,128)} %own_ref.1, s32[1,128]{1,0:T(1,128)} %slot_ref.1, f32[1024,128]{1,0:T(8,128)} %bitcast.15, f32[1024,128]{1,0:T(8,128)} %bitcast.16), custom_call_target="tpu_custom_call" | custom-call | tf_op jit(solution)/shard_map/combine/pallas_call | solution.py:524
  49.4 0.8 %slice.3 = f32[1024,128]{1,0:T(8,128)} slice(f32[1032,128]{1,0:T(8,128)S(1)} %combine.1), slice={[0:1024], [0:128]} | slice | bytes 1048576 | tf_op jit(solution)/shard_map/slice | solution.py:561

commit v4 on v3

--- a/solution.py
+++ b/solution.py
@@ -12,6 +12,8 @@
 
 COLS = 64
 PAD = 8
+EDGE_COEF = 194
+EDGE = 129
 TILE_HALO = PAD + 2 * COLS
 
 
@@ -155,6 +157,8 @@
     start[halo_rows(5), :] = packs[1, 64:128]
     coef[halo_coef(2), :] = packs[0, 128:192]
     coef[halo_coef(5), :] = packs[1, 128:192]
+    for s, node in ((1, 0), (2, 1), (5, 14), (6, 15)):
+        coef[pl.ds(EDGE_COEF * 8 + s, COLS, stride=8), :] = coef[node_rows(0, node), :]
 
     l1 = lev_ref[0, 0]
     l2 = lev_ref[0, 1]
@@ -227,21 +231,16 @@
         )
         return x + 0.1 * diff * second - drift
 
-    def both_groups(ref, c, target, offset, with_halo):
+    def both_groups(ref, c, target, offset):
         ok = masks(c)
         x0 = ref[tile(PAD + c), :]
         x1 = ref[tile(PAD + COLS + c), :]
-        down0, up1 = x0, x1
-        if with_halo:
-            xh = ref[tile(TILE_HALO + c), :]
-            down0 = jnp.where(sub == 7, pltpu.roll(xh, 6, 0), x0)
-            up1 = jnp.where(sub == 0, pltpu.roll(xh, 2, 0), x1)
         value0 = advance(
             PAD + c, x0, pltpu.roll(jnp.where(sub == 0, x1, x0), 7, 0),
-            pltpu.roll(down0, 1, 0), coef[tile(c), :], ok,
+            pltpu.roll(x0, 1, 0), coef[tile(c), :], ok,
         )
         value1 = advance(
-            PAD + COLS + c, x1, pltpu.roll(up1, 7, 0),
+            PAD + COLS + c, x1, pltpu.roll(x1, 7, 0),
             pltpu.roll(jnp.where(sub == 7, x0, x1), 1, 0), coef[tile(COLS + c), :], ok,
         )
         target[tile(offset + c), :] = value0
@@ -249,7 +248,10 @@
 
     for i in range(1024 // shift_chunk):
         shift_lanes(start, PAD * 8 + i * shift_chunk)
-    unrolled(COLS, 2, lambda c: both_groups(start, c, mid, PAD, False))
+    unrolled(COLS, 2, lambda c: both_groups(start, c, mid, PAD))
+    for i in range(1024 // shift_chunk):
+        shift_lanes(mid, PAD * 8 + i * shift_chunk)
+    unrolled(COLS, 2, lambda c: both_groups(mid, c, stepped, 0))
 
     pl.semaphore_wait(barrier, 127)
 
@@ -308,6 +310,25 @@
     here = here.astype(BF16)
     after = after.astype(BF16)
 
+    straddles = jnp.where(both > 7, jnp.where(l1 < 7, 1, 0), jnp.where(both == 6, 1, 0))
+    mask_a = jnp.where(both > 7, skip3 - 1, COLS - 1)
+    no_next = jnp.where(straddles == 1, mask_a, 0)
+    limit_a = jnp.where(both > 7, span2, span3)
+    mask_b = jnp.where(both > 7, COLS - skip3, 0)
+    inside = lane < limit_a
+    chunk = 128
+
+    def lane_part(base_row, i):
+        at = base_row + i * chunk
+        x = stepped[pl.ds(at, chunk), :]
+        beyond = stepped[pl.ds(at + 8, chunk), :]
+        column = jnp.right_shift(i * chunk + lax.broadcasted_iota(I32, (chunk, 128), 0), 3) & (COLS - 1)
+        beyond = jnp.where((column & no_next) != no_next, beyond, 0.0)
+        lanes_done[pl.ds(at, chunk), :] = dot_split(x, here) + dot_split(beyond, after)
+
+    for i in range(1024 // chunk):
+        lane_part(0, i)
+
     @pl.when(d < 7)
     def _():
         down().wait_recv()
@@ -335,27 +356,28 @@
     for i in range(512 // shift_chunk):
         shift_lanes(start, halo + i * shift_chunk)
     unrolled(COLS, 4, first_halo)
-    mid[node_rows(base, 0), :] = mid[halo_rows(2), :]
-    mid[node_rows(base, 15), :] = mid[halo_rows(5), :]
-    for i in range(1024 // shift_chunk):
-        shift_lanes(mid, PAD * 8 + i * shift_chunk)
-    unrolled(COLS, 2, lambda c: both_groups(mid, c, stepped, 0, True))
-
-    straddles = jnp.where(both > 7, jnp.where(l1 < 7, 1, 0), jnp.where(both == 6, 1, 0))
-    mask_a = jnp.where(both > 7, skip3 - 1, COLS - 1)
-    no_next = jnp.where(straddles == 1, mask_a, 0)
-    limit_a = jnp.where(both > 7, span2, span3)
-    mask_b = jnp.where(both > 7, COLS - skip3, 0)
-    inside = lane < limit_a
-    chunk = 128
-
-    def lane_part(i):
-        at = i * chunk
-        x = stepped[pl.ds(at, chunk), :]
-        beyond = stepped[pl.ds(at + 8, chunk), :]
-        column = jnp.right_shift(at + lax.broadcasted_iota(I32, (chunk, 128), 0), 3)
-        beyond = jnp.where((column & no_next) != no_next, beyond, 0.0)
-        lanes_done[pl.ds(at, chunk), :] = dot_split(x, here) + dot_split(beyond, after)
+    for s, source_rows in enumerate(
+        (
+            halo_rows(1), halo_rows(2), node_rows(base, 1), node_rows(base, 2),
+            node_rows(base, 13), node_rows(base, 14), halo_rows(5), halo_rows(6),
+        )
+    ):
+        start[halo_rows(s), :] = mid[source_rows, :]
+    for i in range(512 // shift_chunk):
+        shift_lanes(start, halo + i * shift_chunk)
+
+    def second_edge(c):
+        xh = start[tile(TILE_HALO + c), :]
+        stepped[tile(EDGE + c), :] = advance(
+            TILE_HALO + c, xh, pltpu.roll(xh, 7, 0), pltpu.roll(xh, 1, 0),
+            coef[tile(EDGE_COEF + c), :], masks(c),
+        )
+
+    unrolled(COLS, 4, second_edge)
+    for i in range(512 // chunk):
+        lane_part(EDGE * 8, i)
+    for s, node in ((1, 0), (2, 1), (5, 14), (6, 15)):
+        lanes_done[node_rows(0, node), :] = lanes_done[pl.ds(EDGE * 8 + s, COLS, stride=8), :]
 
     nothing = 2 * COLS
 
@@ -382,16 +404,34 @@
 
     routes = [(0, d > 0, lax.rem(d + 7, 8)), (1, lax.rem(d, 2) == 0, lax.rem(d + 1, 8))]
     routes += [(1, d == 0, 2), (1, d == 0, 4), (1, d == 4, 6), (2, d == 4, 2)]
-    for i in range(1024 // chunk):
-        lane_part(i)
-    columns(lanes_done, rows_done, mask_a, inside)
-    columns(rows_done, lanes_done, mask_b, None)
-    lead[...] = lanes_done[node_rows(0, 0), :]
+    def column_matrix(mask):
+        to_col = lax.broadcasted_iota(I32, (COLS, COLS), 0)
+        from_col = lax.broadcasted_iota(I32, (COLS, COLS), 1)
+        j = to_col & mask
+        off = j & (-j)
+        lower = from_col == to_col - off
+        upper = (j + off <= mask) & (from_col == to_col + off)
+        return jnp.where((j != 0) & (lower | upper), -0.5, 0.0).astype(BF16)
+
+    def times_rows(matrix, rows):
+        high = rows.astype(BF16)
+        low = (rows - high.astype(F32)).astype(BF16)
+        total = jnp.dot(matrix, low, preferred_element_type=F32)
+        return total + jnp.dot(matrix, high, preferred_element_type=F32)
+
+    first_node = lanes_done[node_rows(0, 0), :]
+    lane_of_row = lax.broadcasted_iota(I32, (COLS, 128), 1)
+    change = times_rows(column_matrix(mask_a), first_node)
+    first_node = first_node + jnp.where(lane_of_row < limit_a, change, 0.0)
+    lead[...] = first_node + times_rows(column_matrix(mask_b), first_node)
     for sent, (slot, condition, target) in enumerate(routes):
 
         @pl.when(condition)
         def _():
             lead_copy(slot, target, sent).start()
+
+    columns(lanes_done, rows_done, mask_a, inside)
+    columns(rows_done, lanes_done, mask_b, None)
 
     odd = (sub & 1) == 1
     two = (sub & 3) == 2
@@ -520,7 +560,7 @@
     vmem = pl.BlockSpec(memory_space=pltpu.VMEM)
     anywhere = pl.BlockSpec(memory_space=pltpu.HBM)
     total_rows = (TILE_HALO + COLS + PAD) * 8
-    rows = [total_rows, total_rows, 1552, 1032, 1032, 1032, 1032]
+    rows = [total_rows, total_rows, 2080, 1560, 1560, 1032, 1032]
     combined = pl.pallas_call(
         combine_kernel,
         out_shape=jax.ShapeDtypeStruct((1032, 128), F32),

time: 50.4 us -> 49.2 us (0.976)
  Pallas kernels: 48.8 us -> 47.6 us
    pallas_call x1, Pallas kernels: 48.8 us -> 47.6 us  [body(): pl.pallas_call(combine_kernel, out_shape=jax.ShapeDtypeStruct((1032, 128)...]
where the time goes in v4:
time: 49.2 us; the launch traced here: 49.1 us
  Pallas kernels  47.6 us (97%)
  local copies, waits for them, and re-layouts  0.83 us (2%)
  between operations  0.66 us (1%)
    pallas_call x1, Pallas kernels, body(): pl.pallas_call(combine_kernel, out_shape=jax.ShapeDtypeStruct((1032, 128)...  47.6 us

profile of v4, /device:TPU:1, one launch (start us, length us, event | category | flops | bytes accessed | tf_op | source)
XLA Modules:
  0.0 49.1 jit_solution(9287141714849949004)
XLA Ops:
  0.7 47.6 %combine.1 = f32[1032,128]{1,0:T(8,128)S(1)} custom-call(s32[1,3]{1,0:T(1,128)} %lev_ref.1, f32[4]{0:T(128)} %vel_ref.1, s32[1]{0:T(128)S(6)} %copy.8.sign_ref, s32[1,128]{1,0:T(1,128)} %own_ref.1, s32[1,128]{1,0:T(1,128)} %slot_ref.1, f32[1024,128]{1,0:T(8,128)} %bitcast.15, f32[1024,128]{1,0:T(8,128)} %bitcast.16), custom_call_target="tpu_custom_call" | custom-call | tf_op jit(solution)/shard_map/combine/pallas_call | solution.py:564
  48.3 0.8 %slice.3 = f32[1024,128]{1,0:T(8,128)} slice(f32[1032,128]{1,0:T(8,128)S(1)} %combine.1), slice={[0:1024], [0:128]} | slice | bytes 1048576 | tf_op jit(solution)/shard_map/slice | solution.py:601

commit v5 on v3

--- a/solution.py
+++ b/solution.py
@@ -12,6 +12,7 @@
 
 COLS = 64
 PAD = 8
+EDGE = 1032
 TILE_HALO = PAD + 2 * COLS
 
 
@@ -117,12 +118,9 @@
     second_one = jnp.minimum(rank, 1)
     index_v[0:1] = 8 * owners + 4 * second_one
     index_v[3:4] = 8 * owners + 4 * (1 - second_one)
-    first_row = (row // 64) * (8 * COLS) + (row % 8) * 64 + (row // 8) % 8
     for r in range(2):
         to_owner = (own_col == col) & (rank_col == r)
-        index_v[1 + r : 2 + r] = jnp.sum(
-            jnp.where(to_owner, first_row, 0), axis=0, keepdims=True
-        )
+        index_v[1 + r : 2 + r] = jnp.sum(jnp.where(to_owner, row, 0), axis=0, keepdims=True)
         of_block = (own_row == row) & (rank_row == r)
         ids = jnp.sum(jnp.where(of_block, slot_row + 1, 0), axis=1, keepdims=True) - 1
         table = jnp.where(col == r, ids, table)
@@ -130,15 +128,10 @@
     fetch = pltpu.make_async_copy(index_v, index_s, load_sem.at[2])
     fetch.start()
 
-    lanes_done[1024:1032] = jnp.zeros((8, 128), F32)
-    rows_done[1024:1032] = jnp.zeros((8, 128), F32)
     halo = TILE_HALO * 8
 
-    def halo_rows(s):
-        return pl.ds(halo + s, COLS, stride=8)
-
-    def halo_coef(s):
-        return pl.ds(1024 + s, COLS, stride=8)
+    def slot_rows(slot, count=1):
+        return pl.ds(halo + slot * COLS, count * COLS)
 
     base = PAD * 8
     load_u.wait()
@@ -149,12 +142,10 @@
     packs[1, 0:64] = start[node_rows(base, 14), :]
     packs[1, 64:128] = start[node_rows(base, 15), :]
     packs[1, 128:192] = coef[node_rows(0, 15), :]
-    start[halo_rows(2), :] = packs[0, 0:64]
-    start[halo_rows(3), :] = packs[0, 64:128]
-    start[halo_rows(4), :] = packs[1, 0:64]
-    start[halo_rows(5), :] = packs[1, 64:128]
-    coef[halo_coef(2), :] = packs[0, 128:192]
-    coef[halo_coef(5), :] = packs[1, 128:192]
+    start[slot_rows(2, 2), :] = packs[0, 0:128]
+    start[slot_rows(4, 2), :] = packs[1, 0:128]
+    coef[1024:1088] = coef[node_rows(0, 1), :]
+    coef[1088:1152] = coef[node_rows(0, 14), :]
 
     l1 = lev_ref[0, 0]
     l2 = lev_ref[0, 1]
@@ -210,16 +201,16 @@
         i3 = jnp.right_shift(cell, both) & last3
         return (i2 != last2, i2 != 0, i3 != last3, i3 != 0)
 
-    def advance(at, x, ahead4, behind4, diff, ok):
-        here = tile(at)
-        p2 = jnp.where(stays2, forth[here, :], forth[tile(at + 1), :])
+    def advance(rows_at, x, ahead4, behind4, diff, ok):
+        here = rows_at(0)
+        p2 = jnp.where(stays2, forth[here, :], forth[rows_at(1), :])
         p2 = jnp.where(ok[0], p2, 0.0)
-        m2 = jnp.where(comes2, back2[here, :], back2[tile(at - 1), :])
+        m2 = jnp.where(comes2, back2[here, :], back2[rows_at(-1), :])
         m2 = jnp.where(ok[1], m2, 0.0)
         half = turned3[here, :]
-        p3 = jnp.where(stays3, half, turned3[tile(at + skip3), :])
+        p3 = jnp.where(stays3, half, turned3[rows_at(skip3), :])
         p3 = jnp.where(ok[2], p3, 0.0)
-        m3 = jnp.where(comes3, half, turned3[tile(at - skip3), :])
+        m3 = jnp.where(comes3, half, turned3[rows_at(-skip3), :])
         m3 = jnp.where(ok[3], m3, 0.0)
         second = (sums[here, :] + (p2 + m2)) + ((p3 + m3) + (ahead4 + behind4)) - 8.0 * x
         drift = (drift1 * diffs[here, :] + drift2 * (p2 - m2)) + (
@@ -227,21 +218,16 @@
         )
         return x + 0.1 * diff * second - drift
 
-    def both_groups(ref, c, target, offset, with_halo):
+    def both_groups(ref, c, target, offset):
         ok = masks(c)
         x0 = ref[tile(PAD + c), :]
         x1 = ref[tile(PAD + COLS + c), :]
-        down0, up1 = x0, x1
-        if with_halo:
-            xh = ref[tile(TILE_HALO + c), :]
-            down0 = jnp.where(sub == 7, pltpu.roll(xh, 6, 0), x0)
-            up1 = jnp.where(sub == 0, pltpu.roll(xh, 2, 0), x1)
         value0 = advance(
-            PAD + c, x0, pltpu.roll(jnp.where(sub == 0, x1, x0), 7, 0),
-            pltpu.roll(down0, 1, 0), coef[tile(c), :], ok,
+            lambda k: tile(PAD + c + k), x0, pltpu.roll(jnp.where(sub == 0, x1, x0), 7, 0),
+            pltpu.roll(x0, 1, 0), coef[tile(c), :], ok,
         )
         value1 = advance(
-            PAD + COLS + c, x1, pltpu.roll(up1, 7, 0),
+            lambda k: tile(PAD + COLS + c + k), x1, pltpu.roll(x1, 7, 0),
             pltpu.roll(jnp.where(sub == 7, x0, x1), 1, 0), coef[tile(COLS + c), :], ok,
         )
         target[tile(offset + c), :] = value0
@@ -249,7 +235,12 @@
 
     for i in range(1024 // shift_chunk):
         shift_lanes(start, PAD * 8 + i * shift_chunk)
-    unrolled(COLS, 2, lambda c: both_groups(start, c, mid, PAD, False))
+    unrolled(COLS, 2, lambda c: both_groups(start, c, mid, PAD))
+    for i in range(1024 // shift_chunk):
+        shift_lanes(mid, PAD * 8 + i * shift_chunk)
+    unrolled(COLS, 2, lambda c: both_groups(mid, c, stepped, 0))
+    for slot, node in ((2, 1), (3, 2), (4, 13), (5, 14)):
+        mid[slot_rows(slot), :] = mid[node_rows(base, node), :]
 
     pl.semaphore_wait(barrier, 127)
 
@@ -308,39 +299,6 @@
     here = here.astype(BF16)
     after = after.astype(BF16)
 
-    @pl.when(d < 7)
-    def _():
-        down().wait_recv()
-
-    @pl.when(d > 0)
-    def _():
-        upward().wait_recv()
-
-    start[halo_rows(0), :] = low_in[0:64]
-    start[halo_rows(1), :] = low_in[64:128]
-    start[halo_rows(6), :] = high_in[0:64]
-    start[halo_rows(7), :] = high_in[64:128]
-    coef[halo_coef(1), :] = low_in[128:192]
-    coef[halo_coef(6), :] = high_in[128:192]
-    outside = jnp.where(d == 0, 1, jnp.where(d == 7, 6, -1))
-
-    def first_halo(c):
-        xh = start[tile(TILE_HALO + c), :]
-        value = advance(
-            TILE_HALO + c, xh, pltpu.roll(xh, 7, 0), pltpu.roll(xh, 1, 0),
-            coef[tile(2 * COLS + c), :], masks(c),
-        )
-        mid[tile(TILE_HALO + c), :] = jnp.where(sub == outside, 0.0, value)
-
-    for i in range(512 // shift_chunk):
-        shift_lanes(start, halo + i * shift_chunk)
-    unrolled(COLS, 4, first_halo)
-    mid[node_rows(base, 0), :] = mid[halo_rows(2), :]
-    mid[node_rows(base, 15), :] = mid[halo_rows(5), :]
-    for i in range(1024 // shift_chunk):
-        shift_lanes(mid, PAD * 8 + i * shift_chunk)
-    unrolled(COLS, 2, lambda c: both_groups(mid, c, stepped, 0, True))
-
     straddles = jnp.where(both > 7, jnp.where(l1 < 7, 1, 0), jnp.where(both == 6, 1, 0))
     mask_a = jnp.where(both > 7, skip3 - 1, COLS - 1)
     no_next = jnp.where(straddles == 1, mask_a, 0)
@@ -349,30 +307,90 @@
     inside = lane < limit_a
     chunk = 128
 
-    def lane_part(i):
-        at = i * chunk
+    def lane_part(base_row, i):
+        at = base_row + i * chunk
         x = stepped[pl.ds(at, chunk), :]
         beyond = stepped[pl.ds(at + 8, chunk), :]
-        column = jnp.right_shift(at + lax.broadcasted_iota(I32, (chunk, 128), 0), 3)
+        column = jnp.right_shift(i * chunk + lax.broadcasted_iota(I32, (chunk, 128), 0), 3) & (COLS - 1)
         beyond = jnp.where((column & no_next) != no_next, beyond, 0.0)
         lanes_done[pl.ds(at, chunk), :] = dot_split(x, here) + dot_split(beyond, after)
 
-    nothing = 2 * COLS
-
-    def columns(source, target, mask, chosen):
-        def step(c):
-            j = c & mask
-            off = j & (-j)
-            has_up = (j != 0) & (j + off <= mask)
-            for t in range(2):
-                lower = jnp.where(j != 0, t * COLS + c - off, nothing)
-                upper = jnp.where(has_up, t * COLS + c + off, nothing)
-                update = 0.5 * (source[tile(lower), :] + source[tile(upper), :])
-                if chosen is not None:
-                    update = jnp.where(chosen, update, 0.0)
-                target[tile(t * COLS + c), :] = source[tile(t * COLS + c), :] - update
-
-        unrolled(COLS, 4, step)
+    for i in range(1024 // chunk):
+        lane_part(0, i)
+
+    to_col = lax.broadcasted_iota(I32, (128, 128), 0)
+    from_col = lax.broadcasted_iota(I32, (128, 128), 1) & (COLS - 1)
+    upper_half = to_col < COLS
+    to_col = to_col & (COLS - 1)
+
+    def column_field(mask):
+        to_field, from_field = to_col & mask, from_col & mask
+        bit = to_field & (-to_field)
+        near = (from_field == to_field - bit) | (from_field == to_field + bit)
+        near = jnp.where((to_field != 0) & near, -0.5, 0.0)
+        return jnp.where(to_field == from_field, 1.0, near)
+
+    same_a = jnp.where((to_col & mask_a) == (from_col & mask_a), 1.0, 0.0)
+    columns_matrix = jnp.where(upper_half, column_field(mask_a), same_a) * column_field(mask_b)
+    columns_matrix = columns_matrix.astype(BF16)
+
+    def columns(rows):
+        high = rows.astype(BF16)
+        low = (rows - high.astype(F32)).astype(BF16)
+        terms = jnp.concatenate([high, low], axis=0)
+        done = jnp.dot(columns_matrix, terms, preferred_element_type=F32)
+        lane_of_row = lax.broadcasted_iota(I32, (COLS, rows.shape[1]), 1) & 127
+        return jnp.where(lane_of_row < limit_a, done[:COLS], done[COLS:])
+
+    def edge_step(ref, moves):
+        for i in range(8):
+            ok = masks(i * 8 + sub)
+            for slot, diff, write in moves:
+                at = halo + slot * COLS + i * 8
+                value = advance(
+                    lambda k: pl.ds(at + k, 8), ref[at : at + 8, :],
+                    ref[at + COLS : at + COLS + 8, :], ref[at - COLS : at - COLS + 8, :],
+                    diff(i * 8), ok,
+                )
+                write(i * 8, value)
+
+    def to_mid(slot, zero_at):
+        def write(i, value):
+            if zero_at is not None:
+                value = jnp.where(d == zero_at, 0.0, value)
+            mid[halo + slot * COLS + i : halo + slot * COLS + i + 8, :] = value
+
+        return write
+
+    def to_stepped(place):
+        def write(i, value):
+            stepped[EDGE + place * COLS + i : EDGE + place * COLS + i + 8, :] = value
+
+        return write
+
+    def lane_edge(place):
+        at = EDGE + place * COLS
+        x = stepped[at : at + 128, :]
+        beyond = stepped[at + 1 : at + 129, :]
+        column = lax.broadcasted_iota(I32, (128, 128), 0) & (COLS - 1)
+        beyond = jnp.where((column & no_next) != no_next, beyond, 0.0)
+        lanes_done[at : at + 128, :] = dot_split(x, here) + dot_split(beyond, after)
+
+    coef0 = lambda i: packs[0, 128 + i : 136 + i, :]
+    coef15 = lambda i: packs[1, 128 + i : 136 + i, :]
+
+    @pl.when(d > 0)
+    def _():
+        upward().wait_recv()
+
+    start[slot_rows(0, 2), :] = low_in[0:128]
+    shift_lanes(start, halo + COLS)
+    below = lambda i: low_in[128 + i : 136 + i, :]
+    edge_step(start, ((1, below, to_mid(0, 0)), (2, coef0, to_mid(1, None))))
+    shift_lanes(mid, halo + COLS)
+    coef1 = lambda i: coef[1024 + i : 1032 + i, :]
+    edge_step(mid, ((1, coef0, to_stepped(0)), (2, coef1, to_stepped(1))))
+    lane_edge(0)
 
     def lead_copy(slot, target, sent):
         return pltpu.make_async_remote_copy(
@@ -382,32 +400,50 @@
 
     routes = [(0, d > 0, lax.rem(d + 7, 8)), (1, lax.rem(d, 2) == 0, lax.rem(d + 1, 8))]
     routes += [(1, d == 0, 2), (1, d == 0, 4), (1, d == 4, 6), (2, d == 4, 2)]
-    for i in range(1024 // chunk):
-        lane_part(i)
-    columns(lanes_done, rows_done, mask_a, inside)
-    columns(rows_done, lanes_done, mask_b, None)
-    lead[...] = lanes_done[node_rows(0, 0), :]
+    lead[...] = columns(lanes_done[EDGE : EDGE + COLS, :])
     for sent, (slot, condition, target) in enumerate(routes):
 
         @pl.when(condition)
         def _():
             lead_copy(slot, target, sent).start()
 
-    odd = (sub & 1) == 1
-    two = (sub & 3) == 2
-    four = sub == 4
-
-    def fourth(c):
-        x0 = lanes_done[tile(c), :]
-        x1 = lanes_done[tile(COLS + c), :]
-        for t, x, y, special in ((0, x0, jnp.where(sub == 0, x1, x0), 0.0), (1, x1, jnp.where(sub == 0, 0.0, x1), x0)):
-            near1 = pltpu.roll(y, 7, 0) + pltpu.roll(x, 1, 0)
-            near2 = pltpu.roll(y, 6, 0) + pltpu.roll(x, 2, 0)
-            near4 = pltpu.roll(y, 4, 0) + pltpu.roll(x, 4, 0)
-            near = jnp.where(odd, near1, jnp.where(two, near2, jnp.where(four, near4, special)))
-            surplus[tile(t * COLS + c), :] = x - 0.5 * near
-
-    unrolled(COLS, 2, fourth)
+    @pl.when(d < 7)
+    def _():
+        down().wait_recv()
+
+    start[slot_rows(6, 2), :] = high_in[0:128]
+    shift_lanes(start, halo + 5 * COLS)
+    above = lambda i: high_in[128 + i : 136 + i, :]
+    edge_step(start, ((5, coef15, to_mid(6, None)), (6, above, to_mid(7, 7))))
+    shift_lanes(mid, halo + 5 * COLS)
+    coef14 = lambda i: coef[1088 + i : 1096 + i, :]
+    edge_step(mid, ((5, coef14, to_stepped(2)), (6, coef15, to_stepped(3))))
+    lane_edge(2)
+
+    places = {0: 0, 1: 1, 14: 2, 15: 3}
+
+    def lanes_of(node):
+        if node in places:
+            at = EDGE + places[node] * COLS
+            return lanes_done[at : at + COLS, :]
+        return lanes_done[node_rows(0, node), :]
+
+    for node in range(0, 16, 2):
+        pair = columns(jnp.concatenate([lanes_of(node), lanes_of(node + 1)], axis=1))
+        rows_done[node * COLS : (node + 1) * COLS, :] = pair[:, :128]
+        rows_done[(node + 1) * COLS : (node + 2) * COLS, :] = pair[:, 128:]
+
+    for i in range(0, COLS, 8):
+        nodes = [rows_done[n * COLS + i : n * COLS + i + 8, :] for n in range(16)]
+        for n in range(16):
+            value = nodes[n]
+            bit = n & (-n)
+            if n:
+                near = nodes[n - bit]
+                if n + bit < 16:
+                    near = near + nodes[n + bit]
+                value = value - 0.5 * near
+            surplus[n * COLS + i : n * COLS + i + 8, :] = value
 
     all_of(slots_out, slots_in, slot_sems, 1).wait_recv()
     ids_col = slots_in[:, 0, :]
@@ -451,12 +487,13 @@
     following = 0.5 * lead_in[0]
     use_next = jnp.where(lax.rem(d, 2) == 1, 1.0, 0.0)
     around = 0.5 * (lead_in[1] + lead_in[2]) + use_next * following
-    surplus[node_rows(0, 0), :] = surplus[node_rows(0, 0), :] - around
+    surplus[0:COLS] = surplus[0:COLS] - around
     for node in (8, 12, 14, 15):
-        surplus[node_rows(0, node), :] = surplus[node_rows(0, node), :] - following
+        at = node * COLS
+        surplus[at : at + COLS] = surplus[at : at + COLS] - following
 
     for o in range(128):
-        of_rank = [surplus[pl.ds(index_s[1 + r, o], 8, stride=8), :] for r in range(2)]
+        of_rank = [surplus[tile(index_s[1 + r, o]), :] for r in range(2)]
         turned = pltpu.roll(of_rank[1], 4, 0)
         out_a[o * 8 : o * 8 + 8, :] = jnp.where(sub < 4, of_rank[0], turned)
         out_b[o * 8 : o * 8 + 8, :] = jnp.where(sub < 4, turned, of_rank[0])
@@ -520,7 +557,7 @@
     vmem = pl.BlockSpec(memory_space=pltpu.VMEM)
     anywhere = pl.BlockSpec(memory_space=pltpu.HBM)
     total_rows = (TILE_HALO + COLS + PAD) * 8
-    rows = [total_rows, total_rows, 1552, 1032, 1032, 1032, 1032]
+    rows = [total_rows, total_rows, 1152, 1296, 1296, 1032, 1032]
     combined = pl.pallas_call(
         combine_kernel,
         out_shape=jax.ShapeDtypeStruct((1032, 128), F32),

time: 50.4 us -> 48.6 us (0.964)
  Pallas kernels: 48.8 us -> 47 us
    pallas_call x1, Pallas kernels: 48.8 us -> 47 us  [body(): pl.pallas_call(combine_kernel, out_shape=jax.ShapeDtypeStruct((1032, 128)...]
where the time goes in v5:
time: 48.6 us; the launch traced here: 48.5 us
  Pallas kernels  47 us (97%)
  local copies, waits for them, and re-layouts  0.83 us (2%)
  between operations  0.66 us (1%)
    pallas_call x1, Pallas kernels, body(): pl.pallas_call(combine_kernel, out_shape=jax.ShapeDtypeStruct((1032, 128)...  47 us

profile of v5, /device:TPU:1, one launch (start us, length us, event | category | flops | bytes accessed | tf_op | source)
XLA Modules:
  0.0 48.5 jit_solution(3436207584839234340)
XLA Ops:
  0.7 47.0 %combine.1 = f32[1032,128]{1,0:T(8,128)S(1)} custom-call(s32[1,3]{1,0:T(1,128)} %lev_ref.1, f32[4]{0:T(128)} %vel_ref.1, s32[1]{0:T(128)S(6)} %copy.8.sign_ref, s32[1,128]{1,0:T(1,128)} %own_ref.1, s32[1,128]{1,0:T(1,128)} %slot_ref.1, f32[1024,128]{1,0:T(8,128)} %bitcast.15, f32[1024,128]{1,0:T(8,128)} %bitcast.16), custom_call_target="tpu_custom_call" | custom-call | tf_op jit(solution)/shard_map/combine/pallas_call | solution.py:561
  47.7 0.8 %slice.3 = f32[1024,128]{1,0:T(8,128)} slice(f32[1032,128]{1,0:T(8,128)S(1)} %combine.1), slice={[0:1024], [0:128]} | slice | bytes 1048576 | tf_op jit(solution)/shard_map/slice | solution.py:598

commit v6 on v5

--- a/solution.py
+++ b/solution.py
@@ -238,10 +238,6 @@
     unrolled(COLS, 2, lambda c: both_groups(start, c, mid, PAD))
     for i in range(1024 // shift_chunk):
         shift_lanes(mid, PAD * 8 + i * shift_chunk)
-    unrolled(COLS, 2, lambda c: both_groups(mid, c, stepped, 0))
-    for slot, node in ((2, 1), (3, 2), (4, 13), (5, 14)):
-        mid[slot_rows(slot), :] = mid[node_rows(base, node), :]
-
     pl.semaphore_wait(barrier, 127)
 
     def down():
@@ -282,7 +278,9 @@
             device_id=(g, lax.rem(d + 1, 8)), device_id_type=MESH,
         )
 
-    send_all(slots_out, slots_in, slot_sems, 1)
+    unrolled(COLS, 2, lambda c: both_groups(mid, c, stepped, 0))
+    for slot, node in ((2, 1), (3, 2), (4, 13), (5, 14)):
+        mid[slot_rows(slot), :] = mid[node_rows(base, node), :]
     fetch.wait()
 
     zero_rows = jnp.zeros((192, 128), F32)
@@ -407,6 +405,8 @@
         def _():
             lead_copy(slot, target, sent).start()
 
+    send_all(slots_out, slots_in, slot_sems, 1)
+
     @pl.when(d < 7)
     def _():
         down().wait_recv()
@@ -444,6 +444,49 @@
                     near = near + nodes[n + bit]
                 value = value - 0.5 * near
             surplus[n * COLS + i : n * COLS + i + 8, :] = value
+
+    zero_lead = jnp.zeros((64, 128), F32)
+
+    @pl.when(d == 7)
+    def _():
+        lead_in[0] = zero_lead
+
+    @pl.when(d == 0)
+    def _():
+        lead_in[1] = zero_lead
+
+    @pl.when(d != 2)
+    def _():
+        lead_in[2] = zero_lead
+
+    @pl.when(d < 7)
+    def _():
+        lead_copy(0, lax.rem(d + 7, 8), 0).wait_recv()
+
+    @pl.when(d > 0)
+    def _():
+        lead_copy(1, lax.rem(d + 1, 8), 0).wait_recv()
+
+    @pl.when(d == 2)
+    def _():
+        lead_copy(2, lax.rem(d + 1, 8), 0).wait_recv()
+
+    following = 0.5 * lead_in[0]
+    use_next = jnp.where(lax.rem(d, 2) == 1, 1.0, 0.0)
+    around = 0.5 * (lead_in[1] + lead_in[2]) + use_next * following
+    surplus[0:COLS] = surplus[0:COLS] - around
+    for node in (8, 12, 14, 15):
+        at = node * COLS
+        surplus[at : at + COLS] = surplus[at : at + COLS] - following
+
+    halves = ((out_a, in_a, ret_a, back_a), (out_b, in_b, ret_b, back_b))
+    for half, (outgoing, arrived, _, _) in enumerate(halves):
+        for o in range(128):
+            of_rank = [surplus[tile(index_s[1 + r, o]), :] for r in range(2)]
+            turned = pltpu.roll(of_rank[1], 4, 0)
+            kept = (sub < 4) if half == 0 else (sub >= 4)
+            outgoing[o * 8 : o * 8 + 8, :] = jnp.where(kept, of_rank[0], turned)
+        send_all(outgoing, arrived, out_sems.at[half], 8)
 
     all_of(slots_out, slots_in, slot_sems, 1).wait_recv()
     ids_col = slots_in[:, 0, :]
@@ -457,50 +500,6 @@
         ]
         equal.append(jnp.concatenate(parts, axis=1))
     equal = jnp.concatenate(equal, axis=0).astype(BF16)
-
-    zero_lead = jnp.zeros((64, 128), F32)
-
-    @pl.when(d == 7)
-    def _():
-        lead_in[0] = zero_lead
-
-    @pl.when(d == 0)
-    def _():
-        lead_in[1] = zero_lead
-
-    @pl.when(d != 2)
-    def _():
-        lead_in[2] = zero_lead
-
-    @pl.when(d < 7)
-    def _():
-        lead_copy(0, lax.rem(d + 7, 8), 0).wait_recv()
-
-    @pl.when(d > 0)
-    def _():
-        lead_copy(1, lax.rem(d + 1, 8), 0).wait_recv()
-
-    @pl.when(d == 2)
-    def _():
-        lead_copy(2, lax.rem(d + 1, 8), 0).wait_recv()
-
-    following = 0.5 * lead_in[0]
-    use_next = jnp.where(lax.rem(d, 2) == 1, 1.0, 0.0)
-    around = 0.5 * (lead_in[1] + lead_in[2]) + use_next * following
-    surplus[0:COLS] = surplus[0:COLS] - around
-    for node in (8, 12, 14, 15):
-        at = node * COLS
-        surplus[at : at + COLS] = surplus[at : at + COLS] - following
-
-    for o in range(128):
-        of_rank = [surplus[tile(index_s[1 + r, o]), :] for r in range(2)]
-        turned = pltpu.roll(of_rank[1], 4, 0)
-        out_a[o * 8 : o * 8 + 8, :] = jnp.where(sub < 4, of_rank[0], turned)
-        out_b[o * 8 : o * 8 + 8, :] = jnp.where(sub < 4, turned, of_rank[0])
-
-    halves = ((out_a, in_a, ret_a, back_a), (out_b, in_b, ret_b, back_b))
-    for half, (outgoing, arrived, _, _) in enumerate(halves):
-        send_all(outgoing, arrived, out_sems.at[half], 8)
 
     for half, (outgoing, arrived, returned, back) in enumerate(halves):
         all_of(outgoing, arrived, out_sems.at[half], 8).wait_recv()

time: 48.6 us -> 46.8 us (0.963)
  Pallas kernels: 47 us -> 45 us
    pallas_call x1, Pallas kernels: 47 us -> 45 us  [body(): pl.pallas_call(combine_kernel, out_shape=jax.ShapeDtypeStruct((1032, 128)...]
where the time goes in v6:
time: 46.8 us; the launch traced here: 46.5 us
  Pallas kernels  45 us (96%)
  local copies, waits for them, and re-layouts  0.83 us (2%)
  between operations  0.66 us (1%)
    pallas_call x1, Pallas kernels, body(): pl.pallas_call(combine_kernel, out_shape=jax.ShapeDtypeStruct((1032, 128)...  45 us

profile of v6, /device:TPU:1, one launch (start us, length us, event | category | flops | bytes accessed | tf_op | source)
XLA Modules:
  0.0 46.5 jit_solution(4331747588491624230)
XLA Ops:
  0.7 45.0 %combine.1 = f32[1032,128]{1,0:T(8,128)S(1)} custom-call(s32[1,3]{1,0:T(1,128)} %lev_ref.1, f32[4]{0:T(128)} %vel_ref.1, s32[1]{0:T(128)S(6)} %copy.8.sign_ref, s32[1,128]{1,0:T(1,128)} %own_ref.1, s32[1,128]{1,0:T(1,128)} %slot_ref.1, f32[1024,128]{1,0:T(8,128)} %bitcast.15, f32[1024,128]{1,0:T(8,128)} %bitcast.16), custom_call_target="tpu_custom_call" | custom-call | tf_op jit(solution)/shard_map/combine/pallas_call | solution.py:560
  45.7 0.8 %slice.3 = f32[1024,128]{1,0:T(8,128)} slice(f32[1032,128]{1,0:T(8,128)S(1)} %combine.1), slice={[0:1024], [0:128]} | slice | bytes 1048576 | tf_op jit(solution)/shard_map/slice | solution.py:597

commit v7 on v6

--- a/solution.py
+++ b/solution.py
@@ -63,6 +63,7 @@
 
 def peer_offsets():
     offsets = [(k // 32, k // 8 % 4, k // 2 % 4, k % 2) for k in range(1, 128)]
+    offsets.sort(key=lambda o: (o[0] * 37 + o[1] * 17 + o[2] * 29 + o[3] * 11) % 23)
     return sorted(offsets, key=lambda o: -sum(min(v, 4 - v) for v in o[:3]))
 
 

time: 46.8 us -> 46.8 us (level)
  no operation moved by 1% of the time
where the time goes in v7:
time: 46.8 us; the launch traced here: 46.5 us
  Pallas kernels  45 us (96%)
  local copies, waits for them, and re-layouts  0.83 us (2%)
  between operations  0.66 us (1%)
    pallas_call x1, Pallas kernels, body(): pl.pallas_call(combine_kernel, out_shape=jax.ShapeDtypeStruct((1032, 128)...  45 us

profile of v7, /device:TPU:1, one launch (start us, length us, event | category | flops | bytes accessed | tf_op | source)
XLA Modules:
  0.0 46.5 jit_solution(8085489108527978455)
XLA Ops:
  0.7 45.0 %combine.1 = f32[1032,128]{1,0:T(8,128)S(1)} custom-call(s32[1,3]{1,0:T(1,128)} %lev_ref.1, f32[4]{0:T(128)} %vel_ref.1, s32[1]{0:T(128)S(6)} %copy.8.sign_ref, s32[1,128]{1,0:T(1,128)} %own_ref.1, s32[1,128]{1,0:T(1,128)} %slot_ref.1, f32[1024,128]{1,0:T(8,128)} %bitcast.15, f32[1024,128]{1,0:T(8,128)} %bitcast.16), custom_call_target="tpu_custom_call" | custom-call | tf_op jit(solution)/shard_map/combine/pallas_call | solution.py:561
  45.7 0.8 %slice.3 = f32[1024,128]{1,0:T(8,128)} slice(f32[1032,128]{1,0:T(8,128)S(1)} %combine.1), slice={[0:1024], [0:128]} | slice | bytes 1048576 | tf_op jit(solution)/shard_map/slice | solution.py:598
